TPU v7x, 32 devices: a whole 2x2x4 slice. The times are simulated.
32 devices in a mesh: seq: 4 (over y, core), ctx: 8 (over z, x).
Axes of the slice: x: 2, y: 2, z: 4, core: 2. Of those that a mesh axis runs over, the one named last changes fastest.
Arguments:
- tokens: bfloat16 [4, 2048, 1152], P('seq', 'ctx'), may hold values from -6 to 6
- prefix: int32 [4], P('seq'), may hold values from 204 to 1024
- gain_one: bfloat16 [1152], P('seq'), may hold values from 0.5 to 1.5
- w_query: bfloat16 [1152, 1152], P('seq', 'ctx'), may hold values from -0.1875 to 0.1875
- w_key: bfloat16 [1152, 384], P('seq', 'ctx'), may hold values from -0.1875 to 0.1875
- value_weight: bfloat16 [1152, 384], P('seq', 'ctx'), may hold values from -0.1875 to 0.1875
- w_out: bfloat16 [1152, 1152], P('seq', 'ctx'), may hold values from -6 to 6
- gain_two: bfloat16 [1152], P('seq'), may hold values from 0.5 to 1.5
- w_gate: bfloat16 [1152, 3072], P('seq', 'ctx'), may hold values from -0.1875 to 0.1875
- w_up: bfloat16 [1152, 3072], P('seq', 'ctx'), may hold values from -0.1875 to 0.1875
- w_down: bfloat16 [3072, 1152], P('seq', 'ctx'), may hold values from -0.109375 to 0.109375
- cotangent: bfloat16 [4, 2048, 1152], P('seq', 'ctx'), may hold values from -6 to 6
Outputs:
- output: bfloat16 [4, 2048, 1152], P('seq', 'ctx')
- input_grad: float32 [4, 2048, 1152], P('seq', 'ctx')
- first_gain_gradient: float32 [1152], P('seq')
- grad_query: float32 [1152, 1152], P('seq', 'ctx')
- grad_key: float32 [1152, 384], P('seq', 'ctx')
- grad_value: float32 [1152, 384], P('seq', 'ctx')
- grad_out: float32 [1152, 1152], P('seq', 'ctx')
- second_gain_gradient: float32 [1152], P('seq')
- grad_gate: float32 [1152, 3072], P('seq', 'ctx')
- grad_up: float32 [1152, 3072], P('seq', 'ctx')
- grad_down: float32 [3072, 1152], P('seq', 'ctx')
All inputs are finite; a program needn't handle non-finite values.
Results may differ from a plain program's by a relative error of at most 0.022.
Values may be sent and summed in bfloat16 or wider, within the bound.
A program may use at most 192 MiB of HBM per device.

v0:
```python
import jax
import jax.numpy as jnp
from jax import lax
from jax.sharding import PartitionSpec as P

QUERY_HEADS = 18
KEY_VALUE_HEADS = 6
HEAD_SIZE = 64


EPSILON = 1e-05
ROTARY_BASE = 10000.0


def rotary_tables(positions, head_width):
    half_width = head_width // 2
    frequency = ROTARY_BASE ** (-jnp.arange(half_width, dtype=jnp.float32) * 2.0 / head_width)
    angles = positions.astype(jnp.float32)[:, None] * frequency[None, :]
    return (jnp.cos(angles)[:, None, :], jnp.sin(angles)[:, None, :])


def apply_rotation(values_in, cosine_table, sine_values):
    half_width = values_in.shape[-1] // 2
    first = values_in[..., :half_width]
    second = values_in[..., half_width:]
    return jnp.concatenate(
        [first * cosine_table - second * sine_values, second * cosine_table + first * sine_values],
        axis=-1,
    )


def inverse_rotation(grads_in, cosine_table, sine_values):
    half_width = grads_in.shape[-1] // 2
    first = grads_in[..., :half_width]
    second = grads_in[..., half_width:]
    return jnp.concatenate(
        [first * cosine_table + second * sine_values, second * cosine_table - first * sine_values],
        axis=-1,
    )


def gather_weights(w_query, w_key, value_weight, w_out, w_gate, w_up, w_down, gain_one, gain_two):
    columns = (
        lax.all_gather(w_query, "ctx", axis=1, tiled=True),
        lax.all_gather(w_key, "ctx", axis=1, tiled=True),
        lax.all_gather(value_weight, "ctx", axis=1, tiled=True),
        lax.all_gather(w_out, "ctx", axis=1, tiled=True),
        lax.all_gather(w_gate, "ctx", axis=1, tiled=True),
        lax.all_gather(w_up, "ctx", axis=1, tiled=True),
        lax.all_gather(w_down, "ctx", axis=1, tiled=True),
    )
    return (
        lax.all_gather(columns[0], "seq", axis=0, tiled=True),
        lax.all_gather(columns[1], "seq", axis=0, tiled=True),
        lax.all_gather(columns[2], "seq", axis=0, tiled=True),
        lax.all_gather(columns[3], "seq", axis=0, tiled=True),
        lax.all_gather(columns[4], "seq", axis=0, tiled=True),
        lax.all_gather(columns[5], "seq", axis=0, tiled=True),
        lax.all_gather(columns[6], "seq", axis=0, tiled=True),
        lax.all_gather(gain_one, "seq", axis=0, tiled=True),
        lax.all_gather(gain_two, "seq", axis=0, tiled=True),
    )


def gather_pairs(key_rotated, value_reduced):
    return (
        lax.all_gather(key_rotated, "ctx", axis=1, tiled=True),
        lax.all_gather(value_reduced, "ctx", axis=1, tiled=True),
    )


def head_major(whole_result, sequence_count):
    sequence_length = whole_result.shape[1]
    return (
        whole_result.reshape(sequence_count, sequence_length, KEY_VALUE_HEADS, HEAD_SIZE)
        .transpose(0, 2, 1, 3)
        .reshape(sequence_count * KEY_VALUE_HEADS, sequence_length, HEAD_SIZE)
    )


def per_device(
    tokens,
    prefix,
    gain_one,
    w_query,
    w_key,
    value_weight,
    w_out,
    gain_two,
    w_gate,
    w_up,
    w_down,
    cotangent,
):
    sequence_count, token_local, model_width = tokens.shape
    sequence_length = token_local * lax.axis_size("ctx")
    number_of_rows = sequence_count * token_local
    queries_per_key_head = QUERY_HEADS // KEY_VALUE_HEADS
    score_scale = HEAD_SIZE ** (-0.5)
    gathered = gather_weights(
        w_query, w_key, value_weight, w_out, w_gate, w_up, w_down, gain_one, gain_two
    )
    full_query, full_key, full_value, full_out, full_gate, full_up, full_down = gathered[:7]
    first_norm = gathered[7].astype(jnp.float32)
    second_norm = gathered[8].astype(jnp.float32)
    input_rows = tokens.reshape(number_of_rows, model_width).astype(jnp.float32)
    first_factor = lax.rsqrt(jnp.mean(input_rows * input_rows, axis=-1, keepdims=True) + EPSILON)
    first_normalized_input = input_rows * first_factor
    normalized_rows = (first_normalized_input * first_norm).astype(jnp.bfloat16)
    query_pre = jnp.dot(normalized_rows, full_query, preferred_element_type=jnp.float32)
    key_prerotation = jnp.dot(normalized_rows, full_key, preferred_element_type=jnp.float32)
    value_reduced = jnp.dot(normalized_rows, full_value, preferred_element_type=jnp.float32).astype(
        jnp.bfloat16
    )
    positions = lax.axis_index("ctx") * token_local + jnp.arange(token_local, dtype=jnp.int32)
    cosine_table, sine_values = rotary_tables(positions, HEAD_SIZE)
    query_rows = apply_rotation(
        query_pre.reshape(sequence_count, token_local, QUERY_HEADS, HEAD_SIZE),
        cosine_table,
        sine_values,
    ).astype(jnp.bfloat16)
    key_rotated = apply_rotation(
        key_prerotation.reshape(sequence_count, token_local, KEY_VALUE_HEADS, HEAD_SIZE),
        cosine_table,
        sine_values,
    ).astype(jnp.bfloat16)
    key_rotated = key_rotated.reshape(sequence_count, token_local, KEY_VALUE_HEADS * HEAD_SIZE)
    value_reduced = value_reduced.reshape(sequence_count, token_local, KEY_VALUE_HEADS * HEAD_SIZE)
    keys_all, values_all = gather_pairs(key_rotated, value_reduced)
    query_block_list = query_rows.reshape(
        sequence_count, token_local, KEY_VALUE_HEADS, queries_per_key_head, HEAD_SIZE
    ).transpose(0, 2, 3, 1, 4)
    query_block_list = query_block_list.reshape(
        sequence_count * KEY_VALUE_HEADS, queries_per_key_head, token_local, HEAD_SIZE
    )
    key_blocks = head_major(keys_all, sequence_count)
    value_blocks = head_major(values_all, sequence_count)
    prefix_repeated = jnp.repeat(prefix, KEY_VALUE_HEADS)
    key_place = jnp.arange(sequence_length, dtype=jnp.int32)

    def visible_for(prefix_len):
        return (key_place[None, :] <= positions[:, None]) | (key_place[None, :] < prefix_len)

    def attend(block_item):
        query_block, key_block, value_block, prefix_len = block_item
        scores = (
            jnp.einsum("gqd,kd->gqk", query_block, key_block, preferred_element_type=jnp.float32)
            * score_scale
        )
        scores = jnp.where(visible_for(prefix_len)[None], scores, -1e30)
        row_max = jnp.max(scores, axis=-1, keepdims=True)
        expo = jnp.exp(scores - row_max)
        total = jnp.sum(expo, axis=-1, keepdims=True)
        probs_low = (expo / total).astype(jnp.bfloat16)
        result = jnp.einsum(
            "gqk,kd->gqd", probs_low, value_block, preferred_element_type=jnp.float32
        )
        return (result.astype(jnp.bfloat16), (row_max + jnp.log(total))[..., 0])

    attention_result_blocks, log_totals = lax.map(
        attend, (query_block_list, key_blocks, value_blocks, prefix_repeated)
    )
    attention_result = attention_result_blocks.reshape(
        sequence_count, KEY_VALUE_HEADS, queries_per_key_head, token_local, HEAD_SIZE
    ).transpose(0, 3, 1, 2, 4)
    attention_result = attention_result.reshape(number_of_rows, QUERY_HEADS * HEAD_SIZE)
    mixed_output = input_rows + jnp.dot(
        attention_result, full_out, preferred_element_type=jnp.float32
    )
    second_factor = lax.rsqrt(
        jnp.mean(mixed_output * mixed_output, axis=-1, keepdims=True) + EPSILON
    )
    second_normalized_input = mixed_output * second_factor
    normalized_second = (second_normalized_input * second_norm).astype(jnp.bfloat16)
    gate = jnp.dot(normalized_second, full_gate, preferred_element_type=jnp.float32)
    up_part = jnp.dot(normalized_second, full_up, preferred_element_type=jnp.float32)
    sigmoid_gate = jax.nn.sigmoid(gate)
    activated = gate * sigmoid_gate
    hidden = (activated * up_part).astype(jnp.bfloat16)
    result_rows = mixed_output + jnp.dot(hidden, full_down, preferred_element_type=jnp.float32)
    output = result_rows.astype(jnp.bfloat16).reshape(sequence_count, token_local, model_width)
    gathered = gather_weights(
        w_query, w_key, value_weight, w_out, w_gate, w_up, w_down, gain_one, gain_two
    )
    full_query, full_key, full_value, full_out, full_gate, full_up, full_down = gathered[:7]
    grad_rows_in = cotangent.reshape(number_of_rows, model_width)
    grad_down = jnp.dot(hidden.T, grad_rows_in, preferred_element_type=jnp.float32)
    dhidden = jnp.dot(grad_rows_in, full_down.T, preferred_element_type=jnp.float32)
    dgate = (dhidden * up_part * sigmoid_gate * (1.0 + gate * (1.0 - sigmoid_gate))).astype(
        jnp.bfloat16
    )
    dup_part = (dhidden * activated).astype(jnp.bfloat16)
    grad_gate = jnp.dot(normalized_second.T, dgate, preferred_element_type=jnp.float32)
    grad_up = jnp.dot(normalized_second.T, dup_part, preferred_element_type=jnp.float32)
    normalized_second_grad = jnp.dot(dgate, full_gate.T, preferred_element_type=jnp.float32)
    normalized_second_grad = normalized_second_grad + jnp.dot(
        dup_part, full_up.T, preferred_element_type=jnp.float32
    )
    second_gain_gradient = jnp.sum(normalized_second_grad * second_normalized_input, axis=0)
    second_scaled = normalized_second_grad * second_norm
    dmixed = grad_rows_in.astype(jnp.float32) + second_factor * (
        second_scaled
        - second_normalized_input
        * jnp.mean(second_scaled * second_normalized_input, axis=-1, keepdims=True)
    )
    dproj = dmixed.astype(jnp.bfloat16)
    grad_out = jnp.dot(attention_result.T, dproj, preferred_element_type=jnp.float32)
    attention_result_grad = jnp.dot(dproj, full_out.T, preferred_element_type=jnp.float32).astype(
        jnp.bfloat16
    )
    attention_result_block_grads = attention_result_grad.reshape(
        sequence_count, token_local, KEY_VALUE_HEADS, queries_per_key_head, HEAD_SIZE
    ).transpose(0, 2, 3, 1, 4)
    attention_result_block_grads = attention_result_block_grads.reshape(
        sequence_count * KEY_VALUE_HEADS, queries_per_key_head, token_local, HEAD_SIZE
    )
    keys_all, values_all = gather_pairs(key_rotated, value_reduced)
    key_blocks = head_major(keys_all, sequence_count)
    value_blocks = head_major(values_all, sequence_count)

    def attend_back(block_item):
        query_block, key_block, value_block, prefix_len, log_total, dout_block = block_item
        scores = (
            jnp.einsum("gqd,kd->gqk", query_block, key_block, preferred_element_type=jnp.float32)
            * score_scale
        )
        visible = visible_for(prefix_len)[None]
        probs = jnp.where(
            visible, jnp.exp(jnp.where(visible, scores, -1e30) - log_total[..., None]), 0.0
        )
        dvalues = jnp.einsum(
            "gqk,gqd->kd",
            probs.astype(jnp.bfloat16),
            dout_block,
            preferred_element_type=jnp.float32,
        )
        dprobs = jnp.einsum(
            "gqd,kd->gqk", dout_block, value_block, preferred_element_type=jnp.float32
        )
        dscores = (probs * (dprobs - jnp.sum(probs * dprobs, axis=-1, keepdims=True))).astype(
            jnp.bfloat16
        )
        dquery = (
            jnp.einsum("gqk,kd->gqd", dscores, key_block, preferred_element_type=jnp.float32)
            * score_scale
        )
        dkeys = (
            jnp.einsum("gqk,gqd->kd", dscores, query_block, preferred_element_type=jnp.float32)
            * score_scale
        )
        return (dquery, dkeys, dvalues)

    query_block_grads, key_block_grads, value_block_grads = lax.map(
        attend_back,
        (
            query_block_list,
            key_blocks,
            value_blocks,
            prefix_repeated,
            log_totals,
            attention_result_block_grads,
        ),
    )
    key_grads_combined = key_block_grads.reshape(
        sequence_count, KEY_VALUE_HEADS, sequence_length, HEAD_SIZE
    ).transpose(0, 2, 1, 3)
    key_grads_combined = key_grads_combined.reshape(
        sequence_count, sequence_length, KEY_VALUE_HEADS * HEAD_SIZE
    )
    value_grads_combined = value_block_grads.reshape(
        sequence_count, KEY_VALUE_HEADS, sequence_length, HEAD_SIZE
    ).transpose(0, 2, 1, 3)
    value_grads_combined = value_grads_combined.reshape(
        sequence_count, sequence_length, KEY_VALUE_HEADS * HEAD_SIZE
    )
    key_grads_local, value_grads_local = (
        lax.psum_scatter(
            key_grads_combined.astype(jnp.bfloat16), "ctx", scatter_dimension=1, tiled=True
        ).astype(jnp.float32),
        lax.psum_scatter(
            value_grads_combined.astype(jnp.bfloat16), "ctx", scatter_dimension=1, tiled=True
        ).astype(jnp.float32),
    )
    key_prerotation_grad = inverse_rotation(
        key_grads_local.reshape(sequence_count, token_local, KEY_VALUE_HEADS, HEAD_SIZE),
        cosine_table,
        sine_values,
    )
    key_prerotation_grad = key_prerotation_grad.astype(jnp.bfloat16).reshape(
        number_of_rows, KEY_VALUE_HEADS * HEAD_SIZE
    )
    value_reduced_grad = value_grads_local.astype(jnp.bfloat16).reshape(
        number_of_rows, KEY_VALUE_HEADS * HEAD_SIZE
    )
    query_row_grads = query_block_grads.reshape(
        sequence_count, KEY_VALUE_HEADS, queries_per_key_head, token_local, HEAD_SIZE
    ).transpose(0, 3, 1, 2, 4)
    query_row_grads = query_row_grads.reshape(sequence_count, token_local, QUERY_HEADS, HEAD_SIZE)
    dquery_pre = (
        inverse_rotation(query_row_grads, cosine_table, sine_values)
        .astype(jnp.bfloat16)
        .reshape(number_of_rows, QUERY_HEADS * HEAD_SIZE)
    )
    grad_query = jnp.dot(normalized_rows.T, dquery_pre, preferred_element_type=jnp.float32)
    grad_key = jnp.dot(normalized_rows.T, key_prerotation_grad, preferred_element_type=jnp.float32)
    grad_value = jnp.dot(normalized_rows.T, value_reduced_grad, preferred_element_type=jnp.float32)
    normalized_grad = jnp.dot(dquery_pre, full_query.T, preferred_element_type=jnp.float32)
    normalized_grad = normalized_grad + jnp.dot(
        key_prerotation_grad, full_key.T, preferred_element_type=jnp.float32
    )
    normalized_grad = normalized_grad + jnp.dot(
        value_reduced_grad, full_value.T, preferred_element_type=jnp.float32
    )
    first_gain_gradient = jnp.sum(normalized_grad * first_normalized_input, axis=0)
    first_scaled = normalized_grad * first_norm
    input_grad = dmixed + first_factor * (
        first_scaled
        - first_normalized_input
        * jnp.mean(first_scaled * first_normalized_input, axis=-1, keepdims=True)
    )
    input_grad = input_grad.reshape(sequence_count, token_local, model_width)
    partial_value = (
        lax.psum_scatter(
            grad_query.astype(jnp.bfloat16), "seq", scatter_dimension=0, tiled=True
        ).astype(jnp.float32),
        lax.psum_scatter(
            grad_key.astype(jnp.bfloat16), "seq", scatter_dimension=0, tiled=True
        ).astype(jnp.float32),
        lax.psum_scatter(
            grad_value.astype(jnp.bfloat16), "seq", scatter_dimension=0, tiled=True
        ).astype(jnp.float32),
        lax.psum_scatter(
            grad_out.astype(jnp.bfloat16), "seq", scatter_dimension=0, tiled=True
        ).astype(jnp.float32),
        lax.psum_scatter(
            grad_gate.astype(jnp.bfloat16), "seq", scatter_dimension=0, tiled=True
        ).astype(jnp.float32),
        lax.psum_scatter(
            grad_up.astype(jnp.bfloat16), "seq", scatter_dimension=0, tiled=True
        ).astype(jnp.float32),
        lax.psum_scatter(
            grad_down.astype(jnp.bfloat16), "seq", scatter_dimension=0, tiled=True
        ).astype(jnp.float32),
        lax.psum_scatter(
            first_gain_gradient.astype(jnp.bfloat16), "seq", scatter_dimension=0, tiled=True
        ).astype(jnp.float32),
        lax.psum_scatter(
            second_gain_gradient.astype(jnp.bfloat16), "seq", scatter_dimension=0, tiled=True
        ).astype(jnp.float32),
    )
    owned = (
        lax.psum_scatter(
            partial_value[0].astype(jnp.bfloat16), "ctx", scatter_dimension=1, tiled=True
        ).astype(jnp.float32),
        lax.psum_scatter(
            partial_value[1].astype(jnp.bfloat16), "ctx", scatter_dimension=1, tiled=True
        ).astype(jnp.float32),
        lax.psum_scatter(
            partial_value[2].astype(jnp.bfloat16), "ctx", scatter_dimension=1, tiled=True
        ).astype(jnp.float32),
        lax.psum_scatter(
            partial_value[3].astype(jnp.bfloat16), "ctx", scatter_dimension=1, tiled=True
        ).astype(jnp.float32),
        lax.psum_scatter(
            partial_value[4].astype(jnp.bfloat16), "ctx", scatter_dimension=1, tiled=True
        ).astype(jnp.float32),
        lax.psum_scatter(
            partial_value[5].astype(jnp.bfloat16), "ctx", scatter_dimension=1, tiled=True
        ).astype(jnp.float32),
        lax.psum_scatter(
            partial_value[6].astype(jnp.bfloat16), "ctx", scatter_dimension=1, tiled=True
        ).astype(jnp.float32),
    )
    gains_owned = lax.psum((partial_value[7], partial_value[8]), "ctx")
    final_grads = owned + gains_owned
    return (
        output,
        input_grad,
        final_grads[7],
        final_grads[0],
        final_grads[1],
        final_grads[2],
        final_grads[3],
        final_grads[8],
        final_grads[4],
        final_grads[5],
        final_grads[6],
    )


def solution(mesh):
    placed = (
        P("seq", "ctx", None),
        P("seq"),
        P("seq"),
        P("seq", "ctx"),
        P("seq", "ctx"),
        P("seq", "ctx"),
        P("seq", "ctx"),
        P("seq"),
        P("seq", "ctx"),
        P("seq", "ctx"),
        P("seq", "ctx"),
        P("seq", "ctx", None),
    )
    return jax.shard_map(
        per_device,
        mesh=mesh,
        in_specs=placed,
        out_specs=(
            P("seq", "ctx", None),
            P("seq", "ctx", None),
            P("seq"),
            P("seq", "ctx"),
            P("seq", "ctx"),
            P("seq", "ctx"),
            P("seq", "ctx"),
            P("seq"),
            P("seq", "ctx"),
            P("seq", "ctx"),
            P("seq", "ctx"),
        ),
        check_vma=False,
    )
```

profile of v0, /device:TPU:0, one launch (start us, length us, event | category | flops | bytes accessed | tf_op | source)
XLA Modules:
  0.0 1528.1 jit_solution(16087369697750162979)
XLA Ops:
  12.5 8.5 all-reduce.6
  21.0 32.1 %all_gather.76 = bf16[288,384]{0,1:T(8,128)(2,1)S(1)} all-gather(bf16[288,48]{0,1:T(8,128)(2,1)} %param.21), channel_id=1, replica_groups=mesh['seq'=4,'ctx'=8] {'ctx'}, dimensions={1}, use_global_device_ids=true | all-gather | bytes 248832 | tf_op jit(solution)/shard_map/all_gather | solution.py:46
  53.5 8.1 all_gather.77
  64.4 33.3 %all_gather.71 = bf16[288,1152]{0,1:T(8,128)(2,1)S(1)} all-gather(bf16[288,144]{0,1:T(8,128)(2,1)S(1)} %copy-done.26), channel_id=1, replica_groups=mesh['seq'=4,'ctx'=8] {'ctx'}, dimensions={1}, use_global_device_ids=true | all-gather | bytes 746496 | tf_op jit(solution)/shard_map/all_gather | solution.py:44
  98.9 31.3 %all_gather.73 = bf16[288,384]{0,1:T(8,128)(2,1)S(1)} all-gather(bf16[288,48]{0,1:T(8,128)(2,1)S(1)} %copy-done.28), channel_id=1, replica_groups=mesh['seq'=4,'ctx'=8] {'ctx'}, dimensions={1}, use_global_device_ids=true | all-gather | bytes 248832 | tf_op jit(solution)/shard_map/all_gather | solution.py:45
  130.4 9.3 all_gather.74
  142.2 36.2 %all_gather.79 = bf16[288,1152]{0,1:T(8,128)(2,1)S(1)} all-gather(bf16[288,144]{0,1:T(8,128)(2,1)S(1)} %copy-done.27), channel_id=1, replica_groups=mesh['seq'=4,'ctx'=8] {'ctx'}, dimensions={1}, use_global_device_ids=true | all-gather | bytes 746496 | tf_op jit(solution)/shard_map/all_gather | solution.py:47
  183.5 39.6 %all-gather.26.cloned.1.call-done = bf16[768,1152]{0,1:T(8,128)(2,1)} async-done(((bf16[768,144]{0,1:T(8,128)(2,1)}), bf16[768,1152]{0,1:T(8,128)(2,1)}) %all-gather.26.cloned.1.call-update) | async-done | bytes 1769488 | tf_op jit(solution)/shard_map/all_gather | solution.py:50
  223.4 26.5 %all-gather.12.cloned.1.call-done = bf16[1152,1152]{1,0:T(8,128)(2,1)} async-done(((bf16[288,1152]{1,0:T(8,128)(2,1)}), bf16[1152,1152]{1,0:T(8,128)(2,1)}) %all-gather.12.cloned.1.call-update) | async-done | bytes 2654224 | tf_op jit(solution)/shard_map/all_gather | solution.py:53
  258.2 39.5 %all-gather.14.cloned.1.call-done = bf16[1,2048,384]{1,2,0:T(8,128)(2,1)} async-done(((bf16[1,256,384]{1,2,0:T(8,128)(2,1)}), bf16[1,2048,384]{1,2,0:T(8,128)(2,1)}) %all-gather.14.cloned.1.call-update) | async-done | bytes 1572880 | tf_op jit(solution)/shard_map/all_gather | solution.py:67
  297.7 52.0 %while.30 = (s32[]{:T(128)}, bf16[6,3,256,64]{2,3,1,0:T(8,128)(2,1)}, f32[6,3,256]{2,1,0:T(4,128)S(1)}, s32[6]{0:T(128)S(1)}, bf16[6,3,256,64]{2,3,1,0:T(8,128)(...) while((s32[]{:T(128)}, ...), condition=%wide.region_4.5_spmd.clone.clone, body=%wide.region_1.4_spmd.clone.clone.sunk | while | flops 422626816 | bytes 21730428 | solution.py:160
  354.8 20.9 %all-gather.20.cloned.1.call-done = bf16[1152,3072]{1,0:T(8,128)(2,1)} async-done(((bf16[288,3072]{1,0:T(8,128)(2,1)}), bf16[1152,3072]{1,0:T(8,128)(2,1)}) %all-gather.20.cloned.1.call-update) | async-done | bytes 7077904 | tf_op jit(solution)/shard_map/all_gather | solution.py:57
  382.6 45.6 %all-gather.24.cloned.1.call-done = bf16[1152,3072]{1,0:T(8,128)(2,1)} async-done(((bf16[288,3072]{1,0:T(8,128)(2,1)}), bf16[1152,3072]{1,0:T(8,128)(2,1)}) %all-gather.24.cloned.1.call-update) | async-done | bytes 7077904 | tf_op jit(solution)/shard_map/all_gather | solution.py:58
  435.2 45.3 %all-gather.28.cloned.1.call-done = bf16[3072,1152]{0,1:T(8,128)(2,1)} async-done(((bf16[768,1152]{0,1:T(8,128)(2,1)}), bf16[3072,1152]{0,1:T(8,128)(2,1)}) %all-gather.28.cloned.1.call-update) | async-done | bytes 7077904 | tf_op jit(solution)/shard_map/all_gather | solution.py:59
  480.5 8.9 multiply_convert_fusion.1
  502.4 92.4 %while.31 = (s32[]{:T(128)}, f32[6,3,256,64]{2,3,1,0:T(8,128)}, bf16[6,2048,64]{1,2,0:T(8,128)(2,1)}, bf16[6,2048,64]{1,2,0:T(8,128)(2,1)}, s32[6]{0:T(128)S(1)}...) while((s32[]{:T(128)}, f32[6,3,256,64]{2,3,1,0:T(8,128)}, ...), condition=%wide.region_9.10_spmd.clone.clone, body=%wide.region_7.9_spmd.clone.clone.sunk | while | flops 1023591936 | bytes 50686100 | solution.py:253
  595.5 65.1 %reduce-scatter.31.cloned.1.call-done = bf16[1,256,384]{1,2,0:T(8,128)(2,1)} async-done(((bf16[1,2048,384]{1,2,0:T(8,128)(2,1)}), bf16[1,256,384]{1,2,0:T(8,128)(2,1)}) %reduce-scatter.31.cloned.1.call-update) | async-done | bytes 196624 | tf_op jit(solution)/shard_map/reduce_scatter | solution.py:277
  663.2 65.6 %reduce-scatter.33.cloned.1.call-done = bf16[1,256,384]{1,2,0:T(8,128)(2,1)} async-done(((bf16[1,2048,384]{1,2,0:T(8,128)(2,1)}), bf16[1,256,384]{1,2,0:T(8,128)(2,1)}) %reduce-scatter.33.cloned.1.call-update) | async-done | bytes 196624 | tf_op jit(solution)/shard_map/reduce_scatter | solution.py:280
  761.4 19.2 %reduce-scatter.39.cloned.1.call-done = bf16[288,384]{1,0:T(8,128)(2,1)} async-done(((bf16[1152,384]{1,0:T(8,128)(2,1)}), bf16[288,384]{1,0:T(8,128)(2,1)}) %reduce-scatter.39.cloned.1.call-update) | async-done | bytes 221200 | tf_op jit(solution)/shard_map/reduce_scatter | solution.py:329
  782.5 35.4 %reduce-scatter.35.cloned.1.call-done = bf16[288,1152]{1,0:T(8,128)(2,1)} async-done(((bf16[1152,1152]{1,0:T(8,128)(2,1)}), bf16[288,1152]{1,0:T(8,128)(2,1)}) %reduce-scatter.35.cloned.1.call-update) | async-done | bytes 663568 | tf_op jit(solution)/shard_map/reduce_scatter | solution.py:323
  820.3 35.1 %reduce-scatter.41.cloned.1.call-done = bf16[288,1152]{1,0:T(8,128)(2,1)} async-done(((bf16[1152,1152]{1,0:T(8,128)(2,1)}), bf16[288,1152]{1,0:T(8,128)(2,1)}) %reduce-scatter.41.cloned.1.call-update) | async-done | bytes 663568 | tf_op jit(solution)/shard_map/reduce_scatter | solution.py:332
  857.8 63.7 %reduce-scatter.43.cloned.1.call-done = bf16[288,3072]{1,0:T(8,128)(2,1)} async-done(((bf16[1152,3072]{1,0:T(8,128)(2,1)}), bf16[288,3072]{1,0:T(8,128)(2,1)}) %reduce-scatter.43.cloned.1.call-update) | async-done | bytes 1769488 | tf_op jit(solution)/shard_map/reduce_scatter | solution.py:335
  925.5 62.2 %reduce-scatter.45.cloned.1.call-done = bf16[288,3072]{1,0:T(8,128)(2,1)} async-done(((bf16[1152,3072]{1,0:T(8,128)(2,1)}), bf16[288,3072]{1,0:T(8,128)(2,1)}) %reduce-scatter.45.cloned.1.call-update) | async-done | bytes 1769488 | tf_op jit(solution)/shard_map/reduce_scatter | solution.py:338
  991.8 62.2 %reduce-scatter.47.cloned.1.call-done = bf16[768,1152]{1,0:T(8,128)(2,1)} async-done(((bf16[3072,1152]{1,0:T(8,128)(2,1)}), bf16[768,1152]{1,0:T(8,128)(2,1)}) %reduce-scatter.47.cloned.1.call-update) | async-done | bytes 1769488 | tf_op jit(solution)/shard_map/reduce_scatter | solution.py:341
  1075.9 22.1 %all-reduce.4 = (f32[288]{0:T(512)}, f32[288]{0:T(512)}) all-reduce(f32[288]{0:T(512)S(1)} %get-tuple-element.346, f32[288]{0:T(512)S(1)} %get-tuple-element.345), channel_id=1, replica_groups=mesh['seq'=4,'ctx'=8] {'ctx'}, use_global_device_ids=true, to_apply=%region_15.16 | all-reduce | flops 576 | bytes 4608 | tf_op jit(solution)/shard_map/psum | solution.py:374
  1099.4 17.5 %reduce-scatter.51.cloned.1.call-done = bf16[48,288]{1,0:T(8,128)(2,1)} async-done(((bf16[384,288]{1,0:T(8,128)(2,1)}), bf16[48,288]{1,0:T(8,128)(2,1)}) %reduce-scatter.51.cloned.1.call-update) | async-done | bytes 27664
  1118.5 60.4 %reduce-scatter.53.cloned.1.call-done = bf16[48,288]{1,0:T(8,128)(2,1)} async-done(((bf16[384,288]{1,0:T(8,128)(2,1)}), bf16[48,288]{1,0:T(8,128)(2,1)}) %reduce-scatter.53.cloned.1.call-update) | async-done | bytes 27664
  1180.4 62.3 %reduce-scatter.49.cloned.1.call-done = bf16[144,288]{1,0:T(8,128)(2,1)} async-done(((bf16[1152,288]{1,0:T(8,128)(2,1)}), bf16[144,288]{1,0:T(8,128)(2,1)}) %reduce-scatter.49.cloned.1.call-update) | async-done | bytes 82960
  1244.6 62.2 %reduce-scatter.55.cloned.1.call-done = bf16[144,288]{1,0:T(8,128)(2,1)} async-done(((bf16[1152,288]{1,0:T(8,128)(2,1)}), bf16[144,288]{1,0:T(8,128)(2,1)}) %reduce-scatter.55.cloned.1.call-update) | async-done | bytes 82960
  1308.6 70.1 %reduce-scatter.57.cloned.1.call-done = bf16[384,288]{1,0:T(8,128)(2,1)} async-done(((bf16[3072,288]{1,0:T(8,128)(2,1)}), bf16[384,288]{1,0:T(8,128)(2,1)}) %reduce-scatter.57.cloned.1.call-update) | async-done | bytes 221200
  1380.6 70.1 %reduce-scatter.59.cloned.1.call-done = bf16[384,288]{1,0:T(8,128)(2,1)} async-done(((bf16[3072,288]{1,0:T(8,128)(2,1)}), bf16[384,288]{1,0:T(8,128)(2,1)}) %reduce-scatter.59.cloned.1.call-update) | async-done | bytes 221200
  1452.6 66.8 %reduce-scatter.61.cloned.1.call-done = bf16[144,768]{1,0:T(8,128)(2,1)} async-done(((bf16[1152,768]{1,0:T(8,128)(2,1)}), bf16[144,768]{1,0:T(8,128)(2,1)}) %reduce-scatter.61.cloned.1.call-update) | async-done | bytes 221200
  (321 shorter events, 285.7 us)
Async XLA Ops:
  7.2 172.4 %all-gather.18.cloned.1.call-start = ((), (), s32[]{:S(2)}) async-start(), calls=%async_computation.19 | async-start | bytes 1990656 | tf_op jit(solution)/shard_map/all_gather | solution.py:48
  7.9 172.4 %all-gather.22.cloned.1.call-start = ((), (), s32[]{:S(2)}) async-start(), calls=%async_computation.21 | async-start | bytes 1990656 | tf_op jit(solution)/shard_map/all_gather | solution.py:49
  8.7 173.1 %all-gather.30.cloned.1.call-start = ((), (), s32[]{:S(2)}) async-start(), calls=%async_computation.34 | async-start | bytes 1769472 | tf_op jit(solution)/shard_map/all_gather | solution.py:68
  21.0 234.1 %copy-start.24 = (f32[1152]{0:T(1024)}, f32[1152]{0:T(1024)S(1)}, u32[]{:S(2)}) copy-start(f32[1152]{0:T(1024)S(1)} %convert_element_type.256) | copy-start | bytes 13828
  53.5 201.6 %copy-start.29 = (f32[256]{0:T(256)}, f32[256]{0:T(256)S(1)}, u32[]{:S(2)}) copy-start(f32[256]{0:T(256)S(1)} %add_rsqrt_fusion.1) | copy-start | bytes 3076
  63.8 159.4 %all-gather.26.cloned.1.call-start = ((), (), s32[]{:S(2)}) async-start(), calls=%async_computation.23 | async-start | bytes 1990656 | tf_op jit(solution)/shard_map/all_gather | solution.py:50
  64.4 185.5 %all-gather.12.cloned.1.call-start = ((), (), s32[]{:S(2)}) async-start(), calls=%async_computation.16 | async-start | bytes 3317760 | tf_op jit(solution)/shard_map/all_gather | solution.py:53
  98.8 198.9 %all-gather.14.cloned.1.call-start = ((), (), s32[]{:S(2)}) async-start(), calls=%async_computation.17 | async-start | bytes 1769472 | tf_op jit(solution)/shard_map/all_gather | solution.py:67
  141.3 116.6 %copy-start.18 = (f32[256,32]{0,1:T(8,128)}, f32[256,32]{0,1:T(8,128)S(1)}, u32[]{:S(2)}) copy-start(f32[256,32]{0,1:T(8,128)S(1)} %get-tuple-element.337) | copy-start | bytes 98308
  141.3 116.6 %copy-start.20 = (f32[256,32]{0,1:T(8,128)}, f32[256,32]{0,1:T(8,128)S(1)}, u32[]{:S(2)}) copy-start(f32[256,32]{0,1:T(8,128)S(1)} %get-tuple-element.338) | copy-start | bytes 98308
  142.1 207.6 %all-gather.16.cloned.1.call-start = ((), (), s32[]{:S(2)}) async-start(), calls=%async_computation.18 | async-start | bytes 3317760 | tf_op jit(solution)/shard_map/all_gather | solution.py:56
  179.5 196.2 %all-gather.20.cloned.1.call-start = ((), (), s32[]{:S(2)}) async-start(), calls=%async_computation.20 | async-start | bytes 8847360 | tf_op jit(solution)/shard_map/all_gather | solution.py:57
  180.3 247.9 %all-gather.24.cloned.1.call-start = ((), (), s32[]{:S(2)}) async-start(), calls=%async_computation.22 | async-start | bytes 8847360 | tf_op jit(solution)/shard_map/all_gather | solution.py:58
  181.0 299.5 %all-gather.28.cloned.1.call-start = ((), (), s32[]{:S(2)}) async-start(), calls=%async_computation.24 | async-start | bytes 8847360 | tf_op jit(solution)/shard_map/all_gather | solution.py:59
  223.1 437.4 %reduce-scatter.31.cloned.1.call-start = ((), (), s32[]{:S(2)}) async-start(), calls=%async_computation.25 | async-start | bytes 1769472 | tf_op jit(solution)/shard_map/reduce_scatter | solution.py:277
  354.8 73.4 %copy-start.3 = (bf16[256,1152]{1,0:T(8,128)(2,1)}, bf16[256,1152]{1,0:T(8,128)(2,1)S(1)}, u32[]{:S(2)}) copy-start(bf16[256,1152]{1,0:T(8,128)(2,1)S(1)} %multiply_convert_fusion.4) | copy-start | bytes 1769476
  382.6 97.9 %copy-start.12 = (bf16[1,256,1152]{2,1,0:T(8,128)(2,1)S(1)}, bf16[1,256,1152]{2,1,0:T(8,128)(2,1)}, u32[]{:S(2)}) copy-start(bf16[1,256,1152]{2,1,0:T(8,128)(2,1)} %param.27) | copy-start | bytes 1769476
  594.8 133.9 %reduce-scatter.33.cloned.1.call-start = ((), (), s32[]{:S(2)}) async-start(), calls=%async_computation.26 | async-start | bytes 1769472 | tf_op jit(solution)/shard_map/reduce_scatter | solution.py:280
  595.4 164.1 %reduce-scatter.37.cloned.1.call-start = ((), (), s32[]{:S(2)}) async-start(), calls=%async_computation.28 | async-start | bytes 1105920 | tf_op jit(solution)/shard_map/reduce_scatter | solution.py:326
  663.1 117.5 %reduce-scatter.39.cloned.1.call-start = ((), (), s32[]{:S(2)}) async-start(), calls=%async_computation.29 | async-start | bytes 1105920 | tf_op jit(solution)/shard_map/reduce_scatter | solution.py:329
  731.2 86.6 %reduce-scatter.35.cloned.1.call-start = ((), (), s32[]{:S(2)}) async-start(), calls=%async_computation.27 | async-start | bytes 3317760 | tf_op jit(solution)/shard_map/reduce_scatter | solution.py:323
  734.1 121.2 %reduce-scatter.41.cloned.1.call-start = ((), (), s32[]{:S(2)}) async-start(), calls=%async_computation.30 | async-start | bytes 3317760 | tf_op jit(solution)/shard_map/reduce_scatter | solution.py:332
  737.7 183.8 %reduce-scatter.43.cloned.1.call-start = ((), (), s32[]{:S(2)}) async-start(), calls=%async_computation.31 | async-start | bytes 8847360 | tf_op jit(solution)/shard_map/reduce_scatter | solution.py:335
  745.1 242.6 %reduce-scatter.45.cloned.1.call-start = ((), (), s32[]{:S(2)}) async-start(), calls=%async_computation.32 | async-start | bytes 8847360 | tf_op jit(solution)/shard_map/reduce_scatter | solution.py:338
  751.8 302.2 %reduce-scatter.47.cloned.1.call-start = ((), (), s32[]{:S(2)}) async-start(), calls=%async_computation.33 | async-start | bytes 8847360 | tf_op jit(solution)/shard_map/reduce_scatter | solution.py:341
  759.4 357.4 %reduce-scatter.51.cloned.1.call-start = ((), (), s32[]{:S(2)}) async-start(), calls=%async_computation.36 | async-start | bytes 331776
  761.3 417.5 %reduce-scatter.53.cloned.1.call-start = ((), (), s32[]{:S(2)}) async-start(), calls=%async_computation.37 | async-start | bytes 331776
  782.4 460.3 %reduce-scatter.49.cloned.1.call-start = ((), (), s32[]{:S(2)}) async-start(), calls=%async_computation.35 | async-start | bytes 995328
  820.2 486.5 %reduce-scatter.55.cloned.1.call-start = ((), (), s32[]{:S(2)}) async-start(), calls=%async_computation.38 | async-start | bytes 995328
  857.7 520.9 %reduce-scatter.57.cloned.1.call-start = ((), (), s32[]{:S(2)}) async-start(), calls=%async_computation.39 | async-start | bytes 2654208
  925.5 525.2 %reduce-scatter.59.cloned.1.call-start = ((), (), s32[]{:S(2)}) async-start(), calls=%async_computation.40 | async-start | bytes 2654208
  991.8 527.6 %reduce-scatter.61.cloned.1.call-start = ((), (), s32[]{:S(2)}) async-start(), calls=%async_computation.41 | async-start | bytes 1990656
  (27 other events, 475.9 us)
Sparse Core Ops, SparseCore 0:
  10.1 51.6 all-gather.17
  63.8 54.9 all-gather.21
  121.6 53.1 all-gather.29
  176.8 46.2 all-gather.25
  225.1 24.7 all-gather.11
  252.4 45.2 all-gather.13
  299.3 23.9 all-gather.15
  324.8 50.8 all-gather.19
  377.3 50.8 all-gather.23
  429.6 50.8 all-gather.27
  594.9 65.5 reduce-scatter.30
  664.2 64.5 reduce-scatter.32
  731.3 22.7 reduce-scatter.36
  756.7 23.8 reduce-scatter.38
  783.0 34.8 reduce-scatter.34
  820.4 34.8 reduce-scatter.40
  857.7 63.6 reduce-scatter.42
  924.0 63.6 reduce-scatter.44
  990.3 63.6 reduce-scatter.46
  1058.1 58.7 reduce-scatter.50
  1121.1 57.6 reduce-scatter.52
  1182.6 60.0 reduce-scatter.48
  1246.5 60.1 reduce-scatter.54
  1310.5 68.0 reduce-scatter.56
  1382.5 68.0 reduce-scatter.58
  1454.4 64.9 reduce-scatter.60
where the time goes:
time: 1530 us
  waiting for transfers between devices  1040 us (68%)
  matrix products  189 us (12%)
  blocking collectives  187 us (12%)
  local copies, waits for them, and re-layouts  60.1 us (4%)
  other arithmetic  34 us (2%)
  between operations  16.8 us (1%)
    unnamed x33, waiting for transfers between devices  413 us
    reduce_scatter x1, waiting for transfers between devices, per_device(): lax.psum_scatter(value_grads_combined.astype(jnp.bfloat16), 'ctx', scatte...  65.6 us
    reduce_scatter x1, waiting for transfers between devices, per_device(): lax.psum_scatter(key_grads_combined.astype(jnp.bfloat16), 'ctx', scatter_...  65.1 us
    reduce_scatter x1, waiting for transfers between devices, per_device(): lax.psum_scatter(grad_gate.astype(jnp.bfloat16), 'seq', scatter_dimension...  63.7 us
    reduce_scatter x1, waiting for transfers between devices, per_device(): lax.psum_scatter(grad_up.astype(jnp.bfloat16), 'seq', scatter_dimension=0...  62.2 us
    reduce_scatter x1, waiting for transfers between devices, per_device(): lax.psum_scatter(grad_down.astype(jnp.bfloat16), 'seq', scatter_dimension...  62.2 us
    all_gather x1, waiting for transfers between devices, gather_weights(): lax.all_gather(columns[5], 'seq', axis=0, tiled=True)  45.6 us
    all_gather x1, waiting for transfers between devices, gather_weights(): lax.all_gather(columns[6], 'seq', axis=0, tiled=True)  45.3 us
  transfers between devices with their start and end apart: 26, of which 21 were waited for; matrix products, arithmetic and copies ran while one was open for 11% of the time, Pallas kernels for 0%

commit v1 on v0

--- a/solution.py
+++ b/solution.py
@@ -1,6 +1,10 @@
+import functools
+
 import jax
 import jax.numpy as jnp
 from jax import lax
+from jax.experimental import pallas as pl
+from jax.experimental.pallas import tpu as pltpu
 from jax.sharding import PartitionSpec as P
 
 QUERY_HEADS = 18
@@ -10,6 +14,14 @@
 
 EPSILON = 1e-05
 ROTARY_BASE = 10000.0
+
+LANES = 128
+Z_SIZE = 4
+FLIPS = ((0, 0, 0), (0, 0, 1), (0, 1, 0), (0, 1, 1), (1, 0, 0), (1, 0, 1), (1, 1, 0), (1, 1, 1))
+VMEM_LIMIT = 66_000_000
+F32 = jnp.float32
+BF16 = jnp.bfloat16
+NT = (((1,), (1,)), ((), ()))
 
 
 def rotary_tables(positions, head_width):
@@ -388,6 +400,741 @@
     )
 
 
+def permute_pairs(axis, step):
+    pairs = []
+    for seq_at in range(4):
+        for ctx_at in range(8):
+            target_seq, target_ctx = seq_at, ctx_at
+            if axis == "core":
+                target_seq = seq_at ^ 1
+            elif axis == "y":
+                target_seq = seq_at ^ 2
+            elif axis == "x":
+                target_ctx = ctx_at ^ 1
+            elif axis == "z":
+                target_ctx = (ctx_at + 2 * step) % 8
+            elif axis == "z_flip":
+                target_ctx = ctx_at ^ (2 * step)
+            pairs.append((seq_at * 8 + ctx_at, target_seq * 8 + target_ctx))
+    return pairs
+
+
+def hop(array, axis, step=1):
+    return lax.ppermute(array, ("seq", "ctx"), permute_pairs(axis, step))
+
+
+def gather_shards(shard, order):
+    held = {(0, 0, 0): shard}
+    for axis in order:
+        if axis == "z":
+            for place, array in list(held.items()):
+                ring = [array]
+                for _ in range(Z_SIZE - 1):
+                    ring.append(hop(ring[-1], "z", 1))
+                held[place] = jnp.stack(ring)
+        else:
+            at = ("x", "y", "core").index(axis)
+            for place, array in list(held.items()):
+                held[place[:at] + (1,) + place[at + 1 :]] = hop(array, axis)
+    return [held[flip] for flip in FLIPS]
+
+
+def add_pair(left, right):
+    return (left.astype(F32) + right.astype(F32)).astype(BF16)
+
+
+def scatter_ring(array):
+    total = array[Z_SIZE - 1]
+    for t in range(Z_SIZE - 2, -1, -1):
+        arrived = hop(total, "z", -1)
+        if t:
+            total = add_pair(array[t], arrived)
+        else:
+            total = array[0].astype(F32) + arrived.astype(F32)
+    return total
+
+
+def scatter_rest(near, far, first):
+    second = "x" if first == "y" else "y"
+    arrived = hop(far, first)
+    far_two = add_pair(near[:, 1], arrived[:, 1])
+    near_two = add_pair(near[:, 0], arrived[:, 0])
+    return scatter_ring(add_pair(near_two, hop(far_two, second)))
+
+
+def sum_everywhere(vector):
+    for axis, step in (("core", 1), ("y", 1), ("x", 1), ("z_flip", 1), ("z_flip", 2)):
+        vector = vector + hop(vector, axis, step)
+    return vector
+
+
+def my_place():
+    seq_at, ctx_at = lax.axis_index("seq"), lax.axis_index("ctx")
+    return ctx_at // 2, lax.rem(ctx_at, 2), seq_at // 2, lax.rem(seq_at, 2)
+
+
+def flipped(at, flip):
+    return 1 - at if flip else at
+
+
+def block_copies(arrays, buffer, sems, column_major):
+    z, x, y, core = my_place()
+    copies = {}
+    for number, (dx, dy, dcore) in enumerate(FLIPS):
+        row, column = flipped(y, dy) * 2 + flipped(core, dcore), flipped(x, dx)
+        for t in range(Z_SIZE):
+            ctx_block = lax.rem(z - t + Z_SIZE, Z_SIZE) * 2 + column
+            target = buffer.at[ctx_block, row] if column_major else buffer.at[row, ctx_block]
+            copies[t, dx, dy, dcore] = pltpu.make_async_copy(
+                arrays[number].at[t], target, sems.at[number * Z_SIZE + t]
+            )
+    return copies
+
+
+def lane_ids(rows):
+    return lax.broadcasted_iota(jnp.int32, (rows, LANES), 1)
+
+
+def rotate_halves(tile, cosine, sine):
+    lower = lax.rem(lane_ids(tile.shape[0]), HEAD_SIZE) < HEAD_SIZE // 2
+    swapped = jnp.where(
+        lower, pltpu.roll(tile, LANES - HEAD_SIZE // 2, 1), pltpu.roll(tile, HEAD_SIZE // 2, 1)
+    )
+    return tile * cosine + swapped * sine
+
+
+def pair_tiles(natural):
+    lower = lane_ids(natural[0].shape[0]) < HEAD_SIZE
+    tiles = []
+    for pair in range(3):
+        for member in range(3):
+            one, two = 6 * pair + member, 6 * pair + 3 + member
+            left, right = natural[one // 2], natural[two // 2]
+            if one % 2:
+                left, right = pltpu.roll(left, HEAD_SIZE, 1), pltpu.roll(right, HEAD_SIZE, 1)
+            tiles.append(jnp.where(lower, left, right))
+    return tiles
+
+
+def natural_tiles(paired):
+    lower = lane_ids(paired[0].shape[0]) < HEAD_SIZE
+    tiles = []
+    for at in range(9):
+        sides = []
+        for side in range(2):
+            head = 2 * at + side
+            tile = paired[head // 6 * 3 + head % 3]
+            if (head % 6) // 3 != side:
+                tile = pltpu.roll(tile, HEAD_SIZE, 1)
+            sides.append(tile)
+        tiles.append(jnp.where(lower, sides[0], sides[1]))
+    return tiles
+
+
+def normalized(rows):
+    factor = lax.rsqrt(jnp.mean(rows * rows, axis=-1, keepdims=True) + EPSILON)
+    return factor, rows * factor
+
+
+def project_kernel(tokens, gain, cosine, sine, *refs):
+    weights, (query_out, pair_out, buffer, pieces, wide, sems) = refs[:8], refs[8:]
+    z, x, _, _ = my_place()
+    copies = block_copies(weights, buffer, sems, True)
+    for copy in copies.values():
+        copy.start()
+    _, hat = normalized(tokens[...].astype(F32))
+    rows = (hat * gain[...]).astype(BF16)
+    for t in range(Z_SIZE):
+        for dx in range(2):
+            for dy in range(2):
+                for dcore in range(2):
+                    copies[t, dx, dy, dcore].wait()
+            ctx_block = lax.rem(z - t + Z_SIZE, Z_SIZE) * 2 + flipped(x, dx)
+            matrix = buffer[ctx_block].reshape(tokens.shape[1], buffer.shape[3])
+            pieces[ctx_block] = jnp.dot(rows, matrix, preferred_element_type=F32)
+    q_part, kv_part = 144, 48
+    for at in range(8):
+        wide[:, at * q_part : (at + 1) * q_part] = pieces[at, :, :q_part]
+        wide[:, 1152 + at * kv_part : 1152 + (at + 1) * kv_part] = pieces[at, :, q_part : q_part + kv_part]
+        wide[:, 1536 + at * kv_part : 1536 + (at + 1) * kv_part] = pieces[at, :, q_part + kv_part :]
+    cos_tile, sin_tile = cosine[...], sine[...]
+    natural = [
+        rotate_halves(wide[:, at * LANES : (at + 1) * LANES], cos_tile, sin_tile) * HEAD_SIZE**-0.5
+        for at in range(9)
+    ]
+    for at, tile in enumerate(pair_tiles(natural)):
+        query_out[at] = tile.astype(BF16)
+    for pair in range(3):
+        key_tile = wide[:, 1152 + pair * LANES : 1152 + (pair + 1) * LANES]
+        pair_out[:, 2 * pair * LANES : (2 * pair + 1) * LANES] = rotate_halves(
+            key_tile, cos_tile, sin_tile
+        ).astype(BF16)
+        pair_out[:, (2 * pair + 1) * LANES : (2 * pair + 2) * LANES] = wide[
+            :, 1536 + pair * LANES : 1536 + (pair + 1) * LANES
+        ].astype(BF16)
+
+
+def vmem_specs(count):
+    return [pl.BlockSpec(memory_space=pltpu.VMEM)] * count
+
+
+def any_specs(count):
+    return [pl.BlockSpec(memory_space=pl.ANY)] * count
+
+
+def cost(flops, moved, transcendentals=0):
+    return pl.CostEstimate(flops=int(flops), bytes_accessed=int(moved), transcendentals=int(transcendentals))
+
+
+def params():
+    return pltpu.CompilerParams(vmem_limit_bytes=VMEM_LIMIT)
+
+
+def project(tokens, gain, cosine, sine, weights):
+    rows, width = tokens.shape
+    _, shard_rows, shard_width = weights[0].shape
+    return pl.pallas_call(
+        project_kernel,
+        out_shape=(
+            jax.ShapeDtypeStruct((9, rows, LANES), BF16),
+            jax.ShapeDtypeStruct((rows, 768), BF16),
+        ),
+        in_specs=vmem_specs(4) + any_specs(8),
+        out_specs=tuple(vmem_specs(2)),
+        scratch_shapes=[
+            pltpu.VMEM((8, 4, shard_rows, shard_width), BF16),
+            pltpu.VMEM((8, rows, shard_width), F32),
+            pltpu.VMEM((rows, 1920), F32),
+            pltpu.SemaphoreType.DMA((32,)),
+        ],
+        compiler_params=params(),
+        cost_estimate=cost(2 * rows * width * 1920, 6e6),
+        name="project",
+    )(tokens, gain, cosine, sine, *weights)
+
+
+def slot_start(number):
+    z, x, _, _ = my_place()
+    return (lax.rem(z - number // 2 + Z_SIZE, Z_SIZE) * 2 + flipped(x, number % 2)) * 256
+
+
+def masked_pair(block, half, other):
+    inside = (lane_ids(block.shape[0]) < HEAD_SIZE) == (half == 0)
+    return jnp.where(inside, block.astype(F32), other)
+
+
+def attend_kernel(query, limit, *refs):
+    slots, (out, log_total, keys, values, scores) = refs[:8], refs[8:]
+
+    @pl.when(pl.program_id(1) == 0)
+    def _():
+        for at in range(8):
+            for half in range(2):
+                keys[half, at] = masked_pair(slots[at][:, :LANES], half, 0.0).astype(BF16)
+                values[half, at] = masked_pair(slots[at][:, LANES:], half, 1.0).T.astype(BF16)
+
+    rows = query.shape[1]
+    tile = query[0]
+    key_ids = lax.broadcasted_iota(jnp.int32, (256, rows), 0)
+    parts = []
+    for half in range(2):
+        top = None
+        for at in range(8):
+            part = lax.dot_general(keys[half, at], tile, NT, preferred_element_type=F32)
+            part = jnp.where(key_ids < limit[...] - slot_start(at), part, -1e30)
+            scores[at] = part
+            block_top = jnp.max(part, axis=0, keepdims=True)
+            top = block_top if top is None else jnp.maximum(top, block_top)
+        total = jnp.zeros((LANES, rows), F32)
+        for at in range(8):
+            weight = jnp.exp(scores[at] - top).astype(BF16)
+            total = total + jnp.dot(values[half, at], weight, preferred_element_type=F32)
+        norm = total[HEAD_SIZE : HEAD_SIZE + 1] if half == 0 else total[:1]
+        log_total[0, half : half + 1, :] = top + jnp.log(norm)
+        own = total[:HEAD_SIZE] if half == 0 else total[HEAD_SIZE:]
+        parts.append(own / norm)
+    out[0] = jnp.concatenate(parts, axis=0).T.astype(BF16)
+
+
+def attend(query, limit, slots):
+    rows = query.shape[1]
+    return pl.pallas_call(
+        attend_kernel,
+        grid=(3, 3),
+        out_shape=(
+            jax.ShapeDtypeStruct((9, rows, LANES), BF16),
+            jax.ShapeDtypeStruct((9, 2, rows), F32),
+        ),
+        in_specs=[
+            pl.BlockSpec((1, rows, LANES), lambda p, g: (3 * p + g, 0, 0)),
+            pl.BlockSpec((1, rows), lambda p, g: (0, 0)),
+        ]
+        + [pl.BlockSpec((256, 2 * LANES), lambda p, g: (0, p))] * 8,
+        out_specs=(
+            pl.BlockSpec((1, rows, LANES), lambda p, g: (3 * p + g, 0, 0)),
+            pl.BlockSpec((1, 2, rows), lambda p, g: (3 * p + g, 0, 0)),
+        ),
+        scratch_shapes=[
+            pltpu.VMEM((2, 8, 256, LANES), BF16),
+            pltpu.VMEM((2, 8, LANES, 256), BF16),
+            pltpu.VMEM((8, 256, rows), F32),
+        ],
+        compiler_params=params(),
+        cost_estimate=cost(4 * 18 * rows * 2048 * 128 * 4, 6e6, 18 * rows * 2048),
+        name="attend",
+    )(query, limit, *slots)
+
+
+def attend_back_kernel(query, attended, grad, log_total, limit, cosine, sine, *refs):
+    slots, near, far = refs[:8], refs[8], refs[9:13]
+    query_grad, keys, keys_turned, values, key_sum, value_sum = refs[13:]
+
+    @pl.when(pl.program_id(1) == 0)
+    def _():
+        key_sum[...] = jnp.zeros_like(key_sum)
+        value_sum[...] = jnp.zeros_like(value_sum)
+        for at in range(8):
+            for half in range(2):
+                masked = masked_pair(slots[at][:, :LANES], half, 0.0)
+                keys[half, at] = masked.astype(BF16)
+                keys_turned[half, at] = masked.T.astype(BF16)
+                values[half, at] = masked_pair(slots[at][:, LANES:], half, 0.0).astype(BF16)
+
+    rows = query.shape[1]
+    tile, grad_tile = query[0], grad[0]
+    product = (attended[0].astype(F32) * grad_tile.astype(F32)).T
+    key_ids = lax.broadcasted_iota(jnp.int32, (256, rows), 0)
+    turned = jnp.zeros((LANES, rows), F32)
+    for half in range(2):
+        own = slice(half * HEAD_SIZE, (half + 1) * HEAD_SIZE)
+        shift = jnp.sum(product[own], axis=0, keepdims=True)
+        log_row = log_total[0, half : half + 1, :]
+        query_half = masked_pair(tile, half, 0.0).astype(BF16)
+        grad_half = masked_pair(grad_tile, half, 0.0).astype(BF16)
+        for at in range(8):
+            part = lax.dot_general(keys[half, at], tile, NT, preferred_element_type=F32)
+            part = jnp.where(key_ids < limit[...] - slot_start(at), part, -1e30)
+            probs = jnp.exp(part - log_row)
+            back = lax.dot_general(values[half, at], grad_tile, NT, preferred_element_type=F32)
+            scored = (probs * (back - shift)).astype(BF16)
+            value_sum[at] += jnp.dot(probs.astype(BF16), grad_half, preferred_element_type=F32)
+            key_sum[at] += jnp.dot(scored, query_half, preferred_element_type=F32)
+            turned = turned + jnp.dot(keys_turned[half, at], scored, preferred_element_type=F32)
+    query_grad[0] = rotate_halves(turned.T * HEAD_SIZE**-0.5, cosine[...], -sine[...]).astype(BF16)
+
+    @pl.when(pl.program_id(1) == 2)
+    def _():
+        for at in range(8):
+            ref = far[at // 2] if at % 2 else near.at[at // 2]
+            ref[:, :LANES] = key_sum[at].astype(BF16)
+            ref[:, LANES:] = value_sum[at].astype(BF16)
+
+
+def attend_back(query, attended, grad, log_total, limit, cosine, sine, slots):
+    rows = query.shape[1]
+    tile_spec = pl.BlockSpec((1, rows, LANES), lambda p, g: (3 * p + g, 0, 0))
+    pair_spec = pl.BlockSpec((256, 2 * LANES), lambda p, g: (0, p))
+    table_spec = pl.BlockSpec((rows, LANES), lambda p, g: (0, 0))
+    return pl.pallas_call(
+        attend_back_kernel,
+        grid=(3, 3),
+        out_shape=(jax.ShapeDtypeStruct((4, 256, 768), BF16),)
+        + (jax.ShapeDtypeStruct((256, 768), BF16),) * 4
+        + (jax.ShapeDtypeStruct((9, rows, LANES), BF16),),
+        in_specs=[
+            tile_spec,
+            tile_spec,
+            tile_spec,
+            pl.BlockSpec((1, 2, rows), lambda p, g: (3 * p + g, 0, 0)),
+            pl.BlockSpec((1, rows), lambda p, g: (0, 0)),
+            table_spec,
+            table_spec,
+        ]
+        + [pair_spec] * 8,
+        out_specs=(pl.BlockSpec((4, 256, 2 * LANES), lambda p, g: (0, 0, p)),) + (pair_spec,) * 4 + (tile_spec,),
+        scratch_shapes=[
+            pltpu.VMEM((2, 8, 256, LANES), BF16),
+            pltpu.VMEM((2, 8, LANES, 256), BF16),
+            pltpu.VMEM((2, 8, 256, LANES), BF16),
+            pltpu.VMEM((8, 256, LANES), F32),
+            pltpu.VMEM((8, 256, LANES), F32),
+        ],
+        compiler_params=params(),
+        cost_estimate=cost(4 * 18 * rows * 2048 * 128 * 10, 12e6, 18 * rows * 2048),
+        name="attend_back",
+    )(query, attended, grad, log_total, limit, cosine, sine, *slots)
+
+
+def middle_kernel(tokens, attended, cotangent, gain, *refs):
+    down_in, gate_in, up_in = refs[:8], refs[8:16], refs[16:24]
+    (output, hidden, gate_grad, up_grad, rows_two, mixed_grad, proj_grad, attended_out, attended_grad, gain_grad) = refs[24:34]
+    down, gate_w, up_w, gates, ups, wide, down_sems, gate_sems, up_sems = refs[34:]
+    z, x, _, _ = my_place()
+    down_copies = block_copies(down_in, down, down_sems, False)
+    gate_copies = block_copies(gate_in, gate_w, gate_sems, True)
+    up_copies = block_copies(up_in, up_w, up_sems, True)
+    for copies in (down_copies, gate_copies, up_copies):
+        for copy in copies.values():
+            copy.start()
+    width = tokens.shape[1]
+    for at, tile in enumerate(natural_tiles([attended[at].astype(F32) for at in range(9)])):
+        wide[:, at * LANES : (at + 1) * LANES] = tile
+    for copy in down_copies.values():
+        copy.wait()
+
+    def out_block(row):
+        return down[row, :, :, 768:].reshape(width, 288)
+
+    def down_block(row):
+        return down[row, :, :, :768].reshape(width, 768)
+
+    mixed_grad[...] = tokens[...].astype(F32)
+    for row in range(4):
+        part = wide[:, row * 288 : (row + 1) * 288].astype(BF16)
+        attended_out[row] = part
+        mixed_grad[...] += lax.dot_general(part, out_block(row), NT, preferred_element_type=F32)
+    factor, hat = normalized(mixed_grad[...])
+    gains = gain[...]
+    wide[...] = hat
+    rows_two[...] = (hat * gains).astype(BF16)
+    for t in range(Z_SIZE):
+        for dx in range(2):
+            for dy in range(2):
+                for dcore in range(2):
+                    gate_copies[t, dx, dy, dcore].wait()
+                    up_copies[t, dx, dy, dcore].wait()
+            block = lax.rem(z - t + Z_SIZE, Z_SIZE) * 2 + flipped(x, dx)
+            gates[block] = jnp.dot(rows_two[...], gate_w[block].reshape(width, 384), preferred_element_type=F32)
+            ups[block] = jnp.dot(rows_two[...], up_w[block].reshape(width, 384), preferred_element_type=F32)
+    for row in range(4):
+        for side in range(2):
+            gate, up = gates[2 * row + side], ups[2 * row + side]
+            sigmoid = 1.0 / (1.0 + jnp.exp(-gate))
+            hidden[row, :, side * 384 : (side + 1) * 384] = (gate * sigmoid * up).astype(BF16)
+        mixed_grad[...] += lax.dot_general(hidden[row], down_block(row), NT, preferred_element_type=F32)
+        back = jnp.dot(cotangent[...], down_block(row), preferred_element_type=F32)
+        for side in range(2):
+            gate, up = gates[2 * row + side], ups[2 * row + side]
+            sigmoid = 1.0 / (1.0 + jnp.exp(-gate))
+            part = back[:, side * 384 : (side + 1) * 384]
+            gate_grad[2 * row + side] = (part * up * sigmoid * (1.0 + gate * (1.0 - sigmoid))).astype(BF16)
+            up_grad[2 * row + side] = (part * (gate * sigmoid)).astype(BF16)
+    output[...] = mixed_grad[...].astype(BF16)
+    for block in range(8):
+        grad_two = lax.dot_general(
+            gate_grad[block], gate_w[block].reshape(width, 384), NT, preferred_element_type=F32
+        )
+        grad_two = grad_two + lax.dot_general(
+            up_grad[block], up_w[block].reshape(width, 384), NT, preferred_element_type=F32
+        )
+        mixed_grad[...] = grad_two if block == 0 else mixed_grad[...] + grad_two
+    grad_two, hat = mixed_grad[...], wide[...]
+    gain_grad[...] = jnp.sum(grad_two * hat, axis=0, keepdims=True)
+    scaled = grad_two * gains
+    total = cotangent[...].astype(F32) + factor * (
+        scaled - hat * jnp.mean(scaled * hat, axis=-1, keepdims=True)
+    )
+    mixed_grad[...] = total
+    proj_grad[...] = total.astype(BF16)
+    for row in range(4):
+        wide[:, row * 288 : (row + 1) * 288] = jnp.dot(
+            proj_grad[...], out_block(row), preferred_element_type=F32
+        )
+    tiles = pair_tiles([wide[:, at * LANES : (at + 1) * LANES] for at in range(9)])
+    for at, tile in enumerate(tiles):
+        attended_grad[at] = tile.astype(BF16)
+
+
+def middle(tokens, attended, cotangent, gain, down, gate, up):
+    rows, width = tokens.shape
+    return pl.pallas_call(
+        middle_kernel,
+        out_shape=(
+            jax.ShapeDtypeStruct((rows, width), BF16),
+            jax.ShapeDtypeStruct((4, rows, 768), BF16),
+            jax.ShapeDtypeStruct((8, rows, 384), BF16),
+            jax.ShapeDtypeStruct((8, rows, 384), BF16),
+            jax.ShapeDtypeStruct((rows, width), BF16),
+            jax.ShapeDtypeStruct((rows, width), F32),
+            jax.ShapeDtypeStruct((rows, width), BF16),
+            jax.ShapeDtypeStruct((4, rows, 288), BF16),
+            jax.ShapeDtypeStruct((9, rows, LANES), BF16),
+            jax.ShapeDtypeStruct((1, width), F32),
+        ),
+        in_specs=vmem_specs(4) + any_specs(24),
+        out_specs=tuple(vmem_specs(10)),
+        scratch_shapes=[
+            pltpu.VMEM((4, 8) + down[0].shape[1:], BF16),
+            pltpu.VMEM((8, 4) + gate[0].shape[1:], BF16),
+            pltpu.VMEM((8, 4) + up[0].shape[1:], BF16),
+            pltpu.VMEM((8, rows, 384), F32),
+            pltpu.VMEM((8, rows, 384), F32),
+            pltpu.VMEM((rows, width), F32),
+            pltpu.SemaphoreType.DMA((32,)),
+            pltpu.SemaphoreType.DMA((32,)),
+            pltpu.SemaphoreType.DMA((32,)),
+        ],
+        compiler_params=params(),
+        cost_estimate=cost(2 * rows * width * (6 * 3072 + 2 * 1152), 4e7),
+        name="middle",
+    )(tokens, attended, cotangent, gain, *down, *gate, *up)
+
+
+def turned_rows(matrix, parts):
+    flat = matrix.astype(F32).T.astype(BF16)
+    return flat.reshape(parts, flat.shape[0] // parts, flat.shape[1])
+
+
+def weight_grad_kernel(keep, first, rows_two, gate_grad, up_grad, hidden, cotangent, proj_grad, attended, *refs):
+    if keep:
+        arrived, refs = refs[:3], refs[3:]
+        near, far, turned = refs[:3], refs[3:6], refs[6:]
+    else:
+        outs, turned = refs[:3], refs[3:]
+    rows_turned, cot_turned, proj_turned = turned
+    z, x, y, core = my_place()
+    t = pl.program_id(0)
+
+    @pl.when(t == 0)
+    def _():
+        rows_turned[...] = turned_rows(rows_two[...], 4)
+        cot_turned[...] = turned_rows(cotangent[...], 8)
+        proj_turned[...] = turned_rows(proj_grad[...], 8)
+
+    target_core = core if keep else 1 - core
+    z_at = lax.rem(z - t + Z_SIZE, Z_SIZE)
+
+    def put(group, dx, dy, value):
+        if not keep:
+            outs[group][0, dx, dy] = value.astype(BF16)
+            return
+        value = (value + arrived[group][0, dx, dy].astype(F32)).astype(BF16)
+        flip, other = (dy, dx) if first[group] == "y" else (dx, dy)
+        (far if flip else near)[group][0, other] = value
+
+    for dx in range(2):
+        ctx_block = z_at * 2 + flipped(x, dx)
+        for dy in range(2):
+            row = flipped(y, dy) * 2 + target_core
+            left = rows_turned[row]
+            put(1, dx, dy, jnp.dot(left, gate_grad[ctx_block], preferred_element_type=F32))
+            put(2, dx, dy, jnp.dot(left, up_grad[ctx_block], preferred_element_type=F32))
+            value = jnp.concatenate(
+                [
+                    jnp.dot(cot_turned[ctx_block], hidden[row], preferred_element_type=F32),
+                    jnp.dot(proj_turned[ctx_block], attended[row], preferred_element_type=F32),
+                ],
+                axis=1,
+            )
+            put(0, dx, dy, value)
+
+
+def weight_grads(keep, first, rows_two, gate_grad, up_grad, hidden, cotangent, proj_grad, attended, arrived=()):
+    rows, width = rows_two.shape
+    shapes = ((144, 1056), (288, 384), (288, 384))
+    both = [(Z_SIZE, 2, 2) + shape for shape in shapes]
+    half = [(Z_SIZE, 2) + shape for shape in shapes]
+
+    def spec(shape):
+        return pl.BlockSpec((1,) + shape[1:], lambda t: (t,) + (0,) * (len(shape) - 1))
+
+    whole = [rows_two, gate_grad, up_grad, hidden, cotangent, proj_grad, attended]
+    out = half + half if keep else both
+    return pl.pallas_call(
+        functools.partial(weight_grad_kernel, keep, first),
+        grid=(Z_SIZE,),
+        out_shape=tuple(jax.ShapeDtypeStruct(shape, BF16) for shape in out),
+        in_specs=[
+            pl.BlockSpec(array.shape, lambda t, rank=array.ndim: (0,) * rank) for array in whole
+        ]
+        + [spec(shape) for shape in (both if keep else [])],
+        out_specs=tuple(spec(shape) for shape in out),
+        scratch_shapes=[
+            pltpu.VMEM((4, 288, rows), BF16),
+            pltpu.VMEM((8, 144, rows), BF16),
+            pltpu.VMEM((8, 144, rows), BF16),
+        ],
+        compiler_params=params(),
+        cost_estimate=cost(rows * width * (3 * 3072 + 1152), 3e7),
+        name="weight_grads_keep" if keep else "weight_grads_send",
+    )(*whole, *arrived)
+
+
+def project_back_kernel(tokens, gain, query_grad, pair_grad, mixed_grad, cosine, sine, *refs):
+    weights = refs[:8]
+    input_grad, gain_grad, send, kept, buffer, pieces, wide, rows_turned, sems = refs[8:]
+    z, x, y, core = my_place()
+    copies = block_copies(weights, buffer, sems, True)
+    for copy in copies.values():
+        copy.start()
+    width = tokens.shape[1]
+    factor, hat = normalized(tokens[...].astype(F32))
+    gains = gain[...]
+    rows_turned[...] = turned_rows((hat * gains).astype(BF16), 4)
+    for at, tile in enumerate(natural_tiles([query_grad[at].astype(F32) for at in range(9)])):
+        wide[:, at * LANES : (at + 1) * LANES] = tile
+    cos_tile, sin_tile = cosine[...], -sine[...]
+    for pair in range(3):
+        key_tile = pair_grad[:, 2 * pair * LANES : (2 * pair + 1) * LANES].astype(F32)
+        wide[:, 1152 + pair * LANES : 1152 + (pair + 1) * LANES] = rotate_halves(key_tile, cos_tile, sin_tile)
+        wide[:, 1536 + pair * LANES : 1536 + (pair + 1) * LANES] = pair_grad[
+            :, (2 * pair + 1) * LANES : (2 * pair + 2) * LANES
+        ].astype(F32)
+    q_part, kv_part = 144, 48
+    for at in range(8):
+        pieces[at] = jnp.concatenate(
+            [
+                wide[:, at * q_part : (at + 1) * q_part],
+                wide[:, 1152 + at * kv_part : 1152 + (at + 1) * kv_part],
+                wide[:, 1536 + at * kv_part : 1536 + (at + 1) * kv_part],
+            ],
+            axis=1,
+        ).astype(BF16)
+    for t in range(Z_SIZE):
+        for dx in range(2):
+            block = lax.rem(z - t + Z_SIZE, Z_SIZE) * 2 + flipped(x, dx)
+            for dy in range(2):
+                for keep in range(2):
+                    row = flipped(y, dy) * 2 + (core if keep else 1 - core)
+                    value = jnp.dot(rows_turned[row], pieces[block], preferred_element_type=F32)
+                    (kept if keep else send)[t, dx, dy] = value.astype(BF16)
+    for copy in copies.values():
+        copy.wait()
+    grad_one = jnp.zeros_like(hat)
+    for block in range(8):
+        grad_one = grad_one + lax.dot_general(
+            pieces[block], buffer[block].reshape(width, 240), NT, preferred_element_type=F32
+        )
+    gain_grad[...] = jnp.sum(grad_one * hat, axis=0, keepdims=True)
+    scaled = grad_one * gains
+    input_grad[...] = mixed_grad[...] + factor * (
+        scaled - hat * jnp.mean(scaled * hat, axis=-1, keepdims=True)
+    )
+
+
+def project_back(tokens, gain, query_grad, pair_grad, mixed_grad, cosine, sine, weights):
+    rows, width = tokens.shape
+    piece = weights[0].shape[1:]
+    return pl.pallas_call(
+        project_back_kernel,
+        out_shape=(
+            jax.ShapeDtypeStruct((rows, width), F32),
+            jax.ShapeDtypeStruct((1, width), F32),
+            jax.ShapeDtypeStruct((Z_SIZE, 2, 2) + piece, BF16),
+            jax.ShapeDtypeStruct((Z_SIZE, 2, 2) + piece, BF16),
+        ),
+        in_specs=vmem_specs(7) + any_specs(8),
+        out_specs=tuple(vmem_specs(4)),
+        scratch_shapes=[
+            pltpu.VMEM((8, 4) + piece, BF16),
+            pltpu.VMEM((8, rows, 240), BF16),
+            pltpu.VMEM((rows, 1920), F32),
+            pltpu.VMEM((4, 288, rows), BF16),
+            pltpu.SemaphoreType.DMA((32,)),
+        ],
+        compiler_params=params(),
+        cost_estimate=cost(4 * rows * width * 1920, 1.4e7),
+        name="project_back",
+    )(tokens, gain, query_grad, pair_grad, mixed_grad, cosine, sine, *weights)
+
+
+def lane_tables(first, rows):
+    half = HEAD_SIZE // 2
+    frequency = ROTARY_BASE ** (-jnp.arange(half, dtype=F32) * 2.0 / HEAD_SIZE)
+    angles = (first + jnp.arange(rows, dtype=jnp.int32)).astype(F32)[:, None] * frequency[None, :]
+    cosine, sine = jnp.cos(angles), jnp.sin(angles)
+    return jnp.tile(cosine, (1, 4)), jnp.tile(jnp.concatenate([-sine, sine], axis=1), (1, 2))
+
+
+def gather_gains(gain_one, gain_two):
+    held = jnp.stack([gain_one, gain_two])
+    near = jnp.stack([held, hop(held, "core")])
+    every = jnp.concatenate([near, hop(near, "y")])
+    order = jnp.arange(4) ^ lax.axis_index("seq")
+    every = jnp.take(every, order, axis=0).astype(F32)
+    return every[:, 0].reshape(1, -1), every[:, 1].reshape(1, -1)
+
+
+def permuted_device(
+    tokens, prefix, gain_one, w_query, w_key, value_weight, w_out, gain_two, w_gate, w_up, w_down, cotangent
+):
+    _, rows, width = tokens.shape
+    tokens, cotangent = tokens[0], cotangent[0]
+    ctx_at, seq_at = lax.axis_index("ctx"), lax.axis_index("seq")
+    first_norm, second_norm = gather_gains(gain_one, gain_two)
+    qkv = gather_shards(jnp.concatenate([w_query, w_key, value_weight], axis=1), ("z", "x", "y", "core"))
+    down = gather_shards(jnp.concatenate([w_down.T, w_out.T], axis=1), ("z", "y", "x", "core"))
+    gate = gather_shards(w_gate, ("x", "z", "y", "core"))
+    up = gather_shards(w_up, ("z", "x", "y", "core"))
+    cosine, sine = lane_tables(ctx_at * rows, rows)
+    limit = jnp.maximum(ctx_at * rows + jnp.arange(rows, dtype=jnp.int32) + 1, prefix[0])[None, :]
+
+    query, pair = project(tokens, first_norm, cosine, sine, qkv)
+    slots, held = [], pair
+    for t in range(Z_SIZE):
+        slots += [held, hop(held, "x")]
+        if t < Z_SIZE - 1:
+            held = hop(held, "z", 1)
+    attended, log_total = attend(query, limit, slots)
+    (
+        output,
+        hidden,
+        gate_grad,
+        up_grad,
+        rows_two,
+        mixed_grad,
+        proj_grad,
+        attended_rows,
+        attended_grad,
+        second_gain_part,
+    ) = middle(tokens, attended, cotangent, second_norm, down, gate, up)
+
+    first = ("x", "y", "x")
+    factors = (rows_two, gate_grad, up_grad, hidden, cotangent, proj_grad, attended_rows)
+    sent = weight_grads(False, first, *factors)
+    arrived = [hop(array, "core") for array in sent]
+    parts = weight_grads(True, first, *factors, arrived)
+    grad_down_out, grad_gate, grad_up = [
+        scatter_rest(parts[at], parts[3 + at], first[at]) for at in range(3)
+    ]
+    second_gain_gradient = sum_everywhere(second_gain_part)
+
+    near, *far, query_grad = attend_back(
+        query, attended, attended_grad, log_total, limit, cosine, sine, slots
+    )
+    total = add_pair(near[3], hop(far[3], "x"))
+    for t in (2, 1, 0):
+        local = near[t].astype(F32) + hop(far[t], "x").astype(F32)
+        total = (local + hop(total, "z", -1).astype(F32)).astype(BF16)
+    input_grad, first_gain_part, qkv_send, qkv_keep = project_back(
+        tokens, first_norm, query_grad, total, mixed_grad, cosine, sine, qkv
+    )
+    qkv_sum = add_pair(qkv_keep, hop(qkv_send, "core"))
+    grad_qkv = scatter_rest(qkv_sum[:, :, 0], qkv_sum[:, :, 1], "y")
+    first_gain_gradient = sum_everywhere(first_gain_part)
+
+    def own_gain(vector):
+        return lax.dynamic_slice(vector[0], (seq_at * 288,), (288,))
+
+    return (
+        output[None],
+        input_grad[None],
+        own_gain(first_gain_gradient),
+        grad_qkv[:, :144],
+        grad_qkv[:, 144:192],
+        grad_qkv[:, 192:],
+        grad_down_out[:, 768:].T,
+        own_gain(second_gain_gradient),
+        grad_gate,
+        grad_up,
+        grad_down_out[:, :768].T,
+    )
+
+
+def permute_plan_fits(mesh, tokens):
+    return dict(mesh.shape) == {"seq": 4, "ctx": 8} and tokens.shape == (4, 2048, 1152)
+
+
 def solution(mesh):
     placed = (
         P("seq", "ctx", None),
@@ -403,22 +1150,29 @@
         P("seq", "ctx"),
         P("seq", "ctx", None),
     )
-    return jax.shard_map(
-        per_device,
-        mesh=mesh,
-        in_specs=placed,
-        out_specs=(
-            P("seq", "ctx", None),
-            P("seq", "ctx", None),
-            P("seq"),
-            P("seq", "ctx"),
-            P("seq", "ctx"),
-            P("seq", "ctx"),
-            P("seq", "ctx"),
-            P("seq"),
-            P("seq", "ctx"),
-            P("seq", "ctx"),
-            P("seq", "ctx"),
-        ),
-        check_vma=False,
-    )
+
+    def mapped(device_function):
+        return jax.shard_map(
+            device_function,
+            mesh=mesh,
+            in_specs=placed,
+            out_specs=(
+                P("seq", "ctx", None),
+                P("seq", "ctx", None),
+                P("seq"),
+                P("seq", "ctx"),
+                P("seq", "ctx"),
+                P("seq", "ctx"),
+                P("seq", "ctx"),
+                P("seq"),
+                P("seq", "ctx"),
+                P("seq", "ctx"),
+                P("seq", "ctx"),
+            ),
+            check_vma=False,
+        )
+
+    def layer(tokens, *rest):
+        return mapped(permuted_device if permute_plan_fits(mesh, tokens) else per_device)(tokens, *rest)
+
+    return layer

time: 1530 us -> 685 us (0.45)
  waiting for transfers between devices: 1040 us -> 394 us
  matrix products: 189 us -> 0 us
  blocking collectives: 187 us -> 0 us
  Pallas kernels: 0 us -> 150 us
  starting transfers between devices: 1.44 us -> 83.4 us
  local copies, waits for them, and re-layouts: 60.1 us -> 13.7 us
    unnamed x33 -> x0, waiting for transfers between devices: 413 us -> none
    reduce_scatter x9 -> x0, waiting for transfers between devices: 408 us -> none  [the longest x1 65.6 us: per_device(): lax.psum_scatter(value_grads_combined.astype(jnp.bfloat16), 'ctx', scatte...]
    ppermute x0 -> x93, waiting for transfers between devices: none -> 394 us  [hop(): return lax.ppermute(array, ('seq', 'ctx'), permute_pairs(axis, step))]
    all_gather x10 -> x0, waiting for transfers between devices: 218 us -> none  [the longest x1 45.6 us: gather_weights(): lax.all_gather(columns[5], 'seq', axis=0, tiled=True)]
    dot_general x63 -> x0, matrix products: 189 us -> none  [the longest x6 22.4 us: attend_back(): jnp.einsum('gqd,kd->gqk', query_block, key_block, preferred_element_type=...]
    pallas_call x0 -> x7, Pallas kernels: none -> 150 us  [the longest x1 41.9 us: attend_back(): pl.pallas_call(attend_back_kernel, grid=(3, 3), out_shape=(jax.ShapeDtype...]
    all_gather x6 -> x0, blocking collectives: 150 us -> none  [the longest x1 36.2 us: gather_weights(): lax.all_gather(w_out, 'ctx', axis=1, tiled=True)]
    ppermute x0 -> x93, starting transfers between devices: none -> 83.4 us  [hop(): return lax.ppermute(array, ('seq', 'ctx'), permute_pairs(axis, step))]
  transfers between devices with their start and end apart: 26 -> 93, of which waited for: 21 -> 52; matrix products, arithmetic and copies ran while one was open for 11% -> 6% of each run, Pallas kernels for 0% -> 10%
where the time goes in v1:
time: 685 us; the launch traced here: 677 us
  waiting for transfers between devices  394 us (58%)
  Pallas kernels  150 us (22%)
  starting transfers between devices  83.4 us (12%)
  other arithmetic  33.6 us (5%)
  local copies, waits for them, and re-layouts  13.7 us (2%)
    ppermute x93, waiting for transfers between devices, hop(): return lax.ppermute(array, ('seq', 'ctx'), permute_pairs(axis, step))  394 us
    ppermute x93, starting transfers between devices, hop(): return lax.ppermute(array, ('seq', 'ctx'), permute_pairs(axis, step))  83.4 us
    pallas_call x1, Pallas kernels, attend_back(): pl.pallas_call(attend_back_kernel, grid=(3, 3), out_shape=(jax.ShapeDtype...  41.9 us
    pallas_call x1, Pallas kernels, middle(): pl.pallas_call(middle_kernel, out_shape=(jax.ShapeDtypeStruct((rows, widt...  41.1 us
    pallas_call x2, Pallas kernels, weight_grads(): pl.pallas_call(functools.partial(weight_grad_kernel, keep, first), grid=(...  24.2 us
    pallas_call x1, Pallas kernels, attend(): pl.pallas_call(attend_kernel, grid=(3, 3), out_shape=(jax.ShapeDtypeStruc...  22.3 us
    convert_element_type x18, other arithmetic, add_pair(): return (left.astype(F32) + right.astype(F32)).astype(BF16)  19.4 us
  transfers between devices with their start and end apart: 93, of which 52 were waited for; matrix products, arithmetic and copies ran while one was open for 6% of the time, Pallas kernels for 10%

profile of v1, /device:TPU:0, one launch (start us, length us, event | category | flops | bytes accessed | tf_op | source)
XLA Modules:
  0.0 677.4 jit_solution(7389471797329142725)
XLA Ops:
  24.9 8.2 %collective-permute-done.42 = bf16[288,384]{1,0:T(8,128)(2,1)S(1)} collective-permute-done((bf16[288,384]{1,0:T(8,128)(2,1)S(1)}, bf16[288,384]{1,0:T(8,128)(2,1)S(1)}, u32[]{:S(2)}, u32[]{:S(2)}) %collective-permute-start.42) | collective-permute-done | bytes 221216 | tf_op jit(solution)/shard_map/ppermute | solution.py:423
  34.4 6.6 collective-permute-done.4
  46.1 6.7 collective-permute-done.43
  62.3 5.4 collective-permute-done.44
  84.5 24.1 %collective-permute-done.10.refs_6_ = bf16[4,288,240]{2,1,0:T(8,128)(2,1)S(1)} collective-permute-done((bf16[4,288,240]{2,1,0:T(8,128)(2,1)S(1)}, bf16[4,288,240]{2,1,0:T(8,128)(2,1)S(1)}, u32[]{:S(2)}, u32[]{:S(2)}) %collective-permute-start.10) | collective-permute-done | bytes 552992 | tf_op jit(solution)/shard_map/ppermute | solution.py:423
  117.7 10.7 %collective-permute-done.48.refs_20_ = bf16[4,288,384]{2,1,0:T(8,128)(2,1)} collective-permute-done((bf16[4,288,384]{2,1,0:T(8,128)(2,1)S(1)}, bf16[4,288,384]{2,1,0:T(8,128)(2,1)}, u32[]{:S(2)}, u32[]{:S(2)}) %collective-permute-start.48) | collective-permute-done | bytes 884768 | tf_op jit(solution)/shard_map/ppermute | solution.py:423
  136.7 15.8 %collective-permute-done.40.refs_14_ = bf16[4,288,384]{2,1,0:T(8,128)(2,1)} collective-permute-done((bf16[4,288,384]{2,1,0:T(8,128)(2,1)}, bf16[4,288,384]{2,1,0:T(8,128)(2,1)}, u32[]{:S(2)}, u32[]{:S(2)}) %collective-permute-start.40) | collective-permute-done | bytes 884768 | tf_op jit(solution)/shard_map/ppermute | solution.py:423
  154.5 9.9 %project.1 = (bf16[9,256,128]{2,1,0:T(8,128)(2,1)}, bf16[256,768]{1,0:T(8,128)(2,1)}) custom-call(bf16[256,1152]{1,0:T(8,128)(2,1)} %bitcast.179, f32[1,1152]{1,0:T(1,128)} %reshape_squeeze.6.gain, f32[256,128]{1,0:T(8,128)} %copy.41.cosine, f32[256,128]{1,0:T(8,128)} %copy.42.sine, bf16[4,288,240]{2,1,0:T(8,128)(2,1)} %copy-done.2, ...), custom_call_target="tpu_custom_call" | custom-call | flops 1132462080 | bytes 6000000 | tf_op jit(solution)/shard_map/project/pallas_call | solution.py:596
  166.3 14.7 %collective-permute-done.23.refs_2_ = bf16[4,144,1056]{2,1,0:T(8,128)(2,1)} collective-permute-done((bf16[4,144,1056]{2,1,0:T(8,128)(2,1)}, bf16[4,144,1056]{2,1,0:T(8,128)(2,1)}, u32[]{:S(2)}, u32[]{:S(2)}) %collective-permute-start.23) | collective-permute-done | bytes 1216544 | tf_op jit(solution)/shard_map/ppermute | solution.py:423
  181.7 12.7 %collective-permute-done.15.refs_4_ = bf16[256,768]{1,0:T(8,128)(2,1)S(1)} collective-permute-done((bf16[256,768]{1,0:T(8,128)(2,1)S(1)}, bf16[256,768]{1,0:T(8,128)(2,1)S(1)}, u32[]{:S(2)}, u32[]{:S(2)}) %collective-permute-start.15) | collective-permute-done | bytes 393248 | tf_op jit(solution)/shard_map/ppermute | solution.py:423
  198.5 8.2 %collective-permute-done.17.refs_6_ = bf16[256,768]{1,0:T(8,128)(2,1)S(1)} collective-permute-done((bf16[256,768]{1,0:T(8,128)(2,1)S(1)}, bf16[256,768]{1,0:T(8,128)(2,1)S(1)}, u32[]{:S(2)}, u32[]{:S(2)}) %collective-permute-start.17) | collective-permute-done | bytes 393248 | tf_op jit(solution)/shard_map/ppermute | solution.py:423
  210.0 12.1 %collective-permute-done.12.refs_1_ = bf16[256,768]{1,0:T(8,128)(2,1)S(1)} collective-permute-done((bf16[256,768]{1,0:T(8,128)(2,1)}, bf16[256,768]{1,0:T(8,128)(2,1)S(1)}, u32[]{:S(2)}, u32[]{:S(2)}) %collective-permute-start.12) | collective-permute-done | bytes 393248 | tf_op jit(solution)/shard_map/ppermute | solution.py:423
  222.1 8.4 %collective-permute-done.14.refs_3_ = bf16[256,768]{1,0:T(8,128)(2,1)S(1)} collective-permute-done((bf16[256,768]{1,0:T(8,128)(2,1)S(1)}, bf16[256,768]{1,0:T(8,128)(2,1)S(1)}, u32[]{:S(2)}, u32[]{:S(2)}) %collective-permute-start.14) | collective-permute-done | bytes 393248 | tf_op jit(solution)/shard_map/ppermute | solution.py:423
  230.5 8.4 %collective-permute-done.16.refs_5_ = bf16[256,768]{1,0:T(8,128)(2,1)S(1)} collective-permute-done((bf16[256,768]{1,0:T(8,128)(2,1)S(1)}, bf16[256,768]{1,0:T(8,128)(2,1)S(1)}, u32[]{:S(2)}, u32[]{:S(2)}) %collective-permute-start.16) | collective-permute-done | bytes 393248 | tf_op jit(solution)/shard_map/ppermute | solution.py:423
  239.5 7.1 %collective-permute-done.18.refs_7_ = bf16[256,768]{1,0:T(8,128)(2,1)} collective-permute-done((bf16[256,768]{1,0:T(8,128)(2,1)S(1)}, bf16[256,768]{1,0:T(8,128)(2,1)}, u32[]{:S(2)}, u32[]{:S(2)}) %collective-permute-start.18) | collective-permute-done | bytes 393248 | tf_op jit(solution)/shard_map/ppermute | solution.py:423
  246.6 22.3 %attend.1 = (bf16[9,256,128]{2,1,0:T(8,128)(2,1)}, f32[9,2,256]{2,1,0:T(2,128)}) custom-call(bf16[9,256,128]{2,1,0:T(8,128)(2,1)} %get-tuple-element.44.query, s32[1,256]{1,0:T(1,128)} %add_maximum_fusion.limit, bf16[256,768]{1,0:T(8,128)(2,1)} %get-tuple-element.45.refs_0_, bf16[256,768]{1,0:T(8,128)(2,1)} %copy-done.28, bf16[256,768]{1,0:T(8,128)(2,1)} %copy-done.25, ...), custom_call_target="tpu_custom_call" | custom-call | flops 19327352832 | bytes 6000000 | tf_op jit(solution)/shard_map/attend/pallas_call | solution.py:661
  269.9 41.1 %middle.1 = (bf16[256,1152]{1,0:T(8,128)(2,1)}, bf16[4,256,768]{2,1,0:T(8,128)(2,1)}, bf16[8,256,384]{2,1,0:T(8,128)(2,1)}, bf16[8,256,384]{2,1,0:T(8,128)(2,1)}...) custom-call(bf16[256,1152]{1,0:T(8,128)(2,1)} %bitcast.180, ...), custom_call_target="tpu_custom_call" | custom-call | flops 12230590464 | bytes 40000000 | tf_op jit(solution)/shard_map/middle/pallas_call | solution.py:850
  310.9 41.9 %attend_back.1 = (bf16[4,256,768]{2,1,0:T(8,128)(2,1)}, bf16[256,768]{1,0:T(8,128)(2,1)}, bf16[256,768]{1,0:T(8,128)(2,1)}, bf16[256,768]{1,0:T(8,128)(2,1)}, bf...) custom-call(bf16[9,256,128]{2,1,0:T(8,128)(2,1)} %get-tuple-element.44.query, ...), custom_call_target="tpu_custom_call" | custom-call | flops 48318382080 | bytes 12000000 | tf_op jit(solution)/shard_map/attend_back/pallas_call | solution.py:738
  354.9 10.1 %collective-permute-done.55 = bf16[256,768]{1,0:T(8,128)(2,1)S(1)} collective-permute-done((bf16[256,768]{1,0:T(8,128)(2,1)}, bf16[256,768]{1,0:T(8,128)(2,1)S(1)}, u32[]{:S(2)}, u32[]{:S(2)}) %collective-permute-start.55) | collective-permute-done | bytes 393248 | tf_op jit(solution)/shard_map/ppermute | solution.py:423
  368.0 5.4 collective-permute-done.54
  381.5 6.5 collective-permute-done.57
  394.1 10.4 %weight_grads_send.1 = (bf16[4,2,2,144,1056]{4,3,2,1,0:T(8,128)(2,1)}, bf16[4,2,2,288,384]{4,3,2,1,0:T(8,128)(2,1)}, bf16[4,2,2,288,384]{4,3,2,1,0:T(8,128)(2,1)}) custom-call(bf16[256,1152]{1,0:T(8,128)(2,1)} %get-tuple-element.61.rows_two, bf16[8,256,384]{2,1,0:T(8,128)(2,1)} %get-tuple-element.62.gate_grad, ...), custom_call_target="tpu_custom_call" | custom-call | flops 3057647616 | bytes 30000000 | tf_op jit(solution)/shard_map/weight_grads_send/pallas_call | solution.py:943
  406.5 10.9 %project_back.1 = (f32[256,1152]{1,0:T(8,128)}, f32[1,1152]{1,0:T(1,128)}, bf16[4,2,2,288,240]{4,3,2,1,0:T(8,128)(2,1)}, bf16[4,2,2,288,240]{4,3,2,1,0:T(8,128)(2,1)}) custom-call(bf16[256,1152]{1,0:T(8,128)(2,1)} %bitcast.181, f32[1,1152]{1,0:T(1,128)} %reshape_squeeze.6.gain, bf16[9,256,128]{2,1,0:T(8,128)(2,1)} %get-tuple-element.50.query_grad, ...), custom_call_target="tpu_custom_call" | custom-call | flops 2264924160 | bytes 14000000 | tf_op jit(solution)/shard_map/project_back/pallas_call | solution.py:1018
  418.5 6.5 collective-permute-done.64
  429.1 26.7 %collective-permute-done.65 = bf16[4,2,288,240]{3,2,1,0:T(8,128)(2,1)S(1)} collective-permute-done((bf16[4,2,288,240]{3,2,1,0:T(8,128)(2,1)S(1)}, bf16[4,2,288,240]{3,2,1,0:T(8,128)(2,1)S(1)}, u32[]{:S(2)}, u32[]{:S(2)}) %collective-permute-start.65) | collective-permute-done | bytes 1105952 | tf_op jit(solution)/shard_map/ppermute | solution.py:423
  457.0 13.8 %weight_grads_keep.1 = (bf16[4,2,144,1056]{3,2,1,0:T(8,128)(2,1)}, bf16[4,2,288,384]{3,2,1,0:T(8,128)(2,1)}, bf16[4,2,288,384]{3,2,1,0:T(8,128)(2,1)}, bf16[4,2,...) custom-call(bf16[256,1152]{1,0:T(8,128)(2,1)} %get-tuple-element.61.rows_two, ...), custom_call_target="tpu_custom_call" | custom-call | flops 3057647616 | bytes 30000000 | tf_op jit(solution)/shard_map/weight_grads_keep/pallas_call | solution.py:943
  476.2 5.1 collective-permute-done.67
  493.3 19.3 %collective-permute-done.79 = f32[1,1152]{1,0:T(1,128)S(1)} collective-permute-done((f32[1,1152]{1,0:T(1,128)S(1)}, f32[1,1152]{1,0:T(1,128)S(1)}, u32[]{:S(2)}, u32[]{:S(2)}) %collective-permute-start.79) | collective-permute-done | bytes 4640 | tf_op jit(solution)/shard_map/ppermute | solution.py:423
  516.5 51.4 %collective-permute-done.80 = f32[1,1152]{1,0:T(1,128)S(1)} collective-permute-done((f32[1,1152]{1,0:T(1,128)S(1)}, f32[1,1152]{1,0:T(1,128)S(1)}, u32[]{:S(2)}, u32[]{:S(2)}) %collective-permute-start.80) | collective-permute-done | bytes 4640 | tf_op jit(solution)/shard_map/ppermute | solution.py:423
  608.8 10.2 %collective-permute-done.89 = bf16[4,288,384]{2,1,0:T(8,128)(2,1)} collective-permute-done((bf16[4,288,384]{2,1,0:T(8,128)(2,1)}, bf16[4,288,384]{2,1,0:T(8,128)(2,1)}, u32[]{:S(2)}, u32[]{:S(2)}) %collective-permute-start.89) | collective-permute-done | bytes 884768 | tf_op jit(solution)/shard_map/ppermute | solution.py:423
  620.9 17.9 %collective-permute-done.74 = bf16[4,144,1056]{2,1,0:T(8,128)(2,1)} collective-permute-done((bf16[4,144,1056]{2,1,0:T(8,128)(2,1)}, bf16[4,144,1056]{2,1,0:T(8,128)(2,1)}, u32[]{:S(2)}, u32[]{:S(2)}) %collective-permute-start.74) | collective-permute-done | bytes 1216544 | tf_op jit(solution)/shard_map/ppermute | solution.py:423
  644.5 7.3 %collective-permute-done.75 = bf16[144,1056]{1,0:T(8,128)(2,1)S(1)} collective-permute-done((bf16[144,1056]{1,0:T(8,128)(2,1)S(1)}, bf16[144,1056]{1,0:T(8,128)(2,1)S(1)}, u32[]{:S(2)}, u32[]{:S(2)}) %collective-permute-start.75) | collective-permute-done | bytes 304160 | tf_op jit(solution)/shard_map/ppermute | solution.py:423
  (304 shorter events, 209.1 us)
Async XLA Ops:
  23.6 34.0 %collective-permute-start.20 = (bf16[144,1056]{1,0:T(8,128)(2,1)S(1)}, bf16[144,1056]{1,0:T(8,128)(2,1)S(1)}, u32[]{:S(2)}, u32[]{:S(2)}) collective-permute-start(bf16[144,1056]{1,0:T(8,128)(2,1)S(1)} %collective-permute-done.19), channel_id=1, source_target_pairs={{0,2},{1,3},{2,4},{3,5},{4,6},{5,7},{6,0},{7,1},{8,10},{9,11},{10,... | collective-permute-start | bytes 912392 | tf_op jit(solution)/shard_map/ppermute | solution.py:423
  44.6 34.2 %collective-permute-start.8 = (bf16[4,288,240]{2,1,0:T(8,128)(2,1)S(1)}, bf16[4,288,240]{2,1,0:T(8,128)(2,1)S(1)}, u32[]{:S(2)}, u32[]{:S(2)}) collective-permute-start(bf16[4,288,240]{2,1,0:T(8,128)(2,1)S(1)} %pad_maximum_fusion.4.refs_0_), channel_id=1, source_target_pairs={{0,1},{1,0},{2,3},{3,2},{4,5},{5,4},{6,7},{7,6},{8,9},{9,8},{10,11... | collective-permute-start | bytes 1658888 | tf_op jit(solution)/shard_map/ppermute | solution.py:423
  52.9 30.2 %collective-permute-start.6 = (bf16[4,288,240]{2,1,0:T(8,128)(2,1)S(1)}, bf16[4,288,240]{2,1,0:T(8,128)(2,1)S(1)}, u32[]{:S(2)}, u32[]{:S(2)}) collective-permute-start(bf16[4,288,240]{2,1,0:T(8,128)(2,1)S(1)} %pad_maximum_fusion.4.refs_0_), channel_id=1, source_target_pairs={{0,16},{1,17},{2,18},{3,19},{4,20},{5,21},{6,22},{7,23},{8,24},{9,... | collective-permute-start | bytes 1658888 | tf_op jit(solution)/shard_map/ppermute | solution.py:423
  77.2 36.4 %collective-permute-start.33 = (bf16[4,288,384]{2,1,0:T(8,128)(2,1)S(1)}, bf16[4,288,384]{2,1,0:T(8,128)(2,1)S(1)}, u32[]{:S(2)}, u32[]{:S(2)}) collective-permute-start(bf16[4,288,384]{2,1,0:T(8,128)(2,1)S(1)} %pad_maximum_fusion.1.refs_8_), channel_id=1, source_target_pairs={{0,16},{1,17},{2,18},{3,19},{4,20},{5,21},{6,22},{7,23},{8,24},{9,... | collective-permute-start | bytes 2654216 | tf_op jit(solution)/shard_map/ppermute | solution.py:423
  78.8 29.9 %collective-permute-start.10 = (bf16[4,288,240]{2,1,0:T(8,128)(2,1)S(1)}, bf16[4,288,240]{2,1,0:T(8,128)(2,1)S(1)}, u32[]{:S(2)}, u32[]{:S(2)}) collective-permute-start(bf16[4,288,240]{2,1,0:T(8,128)(2,1)S(1)} %collective-permute-done.8.refs_4_), channel_id=1, source_target_pairs={{0,16},{1,17},{2,18},{3,19},{4,20},{5,21},{6,22},{7,23},{8,24},{9,... | collective-permute-start | bytes 1658888 | tf_op jit(solution)/shard_map/ppermute | solution.py:423
  83.0 29.5 %collective-permute-start.7 = (bf16[4,288,240]{2,1,0:T(8,128)(2,1)S(1)}, bf16[4,288,240]{2,1,0:T(8,128)(2,1)S(1)}, u32[]{:S(2)}, u32[]{:S(2)}) collective-permute-start(bf16[4,288,240]{2,1,0:T(8,128)(2,1)S(1)} %collective-permute-done.6.refs_2_), channel_id=1, source_target_pairs={{0,8},{1,9},{2,10},{3,11},{4,12},{5,13},{6,14},{7,15},{8,0},{9,1},... | collective-permute-start | bytes 1658888 | tf_op jit(solution)/shard_map/ppermute | solution.py:423
  83.5 31.2 %collective-permute-start.32 = (bf16[4,288,384]{2,1,0:T(8,128)(2,1)S(1)}, bf16[4,288,384]{2,1,0:T(8,128)(2,1)}, u32[]{:S(2)}, u32[]{:S(2)}) collective-permute-start(bf16[4,288,384]{2,1,0:T(8,128)(2,1)S(1)} %pad_maximum_fusion.1.refs_8_), channel_id=1, source_target_pairs={{0,8},{1,9},{2,10},{3,11},{4,12},{5,13},{6,14},{7,15},{8,0},{9,1},... | collective-permute-start | bytes 2654216 | tf_op jit(solution)/shard_map/ppermute | solution.py:423
  113.6 38.9 %collective-permute-start.40 = (bf16[4,288,384]{2,1,0:T(8,128)(2,1)}, bf16[4,288,384]{2,1,0:T(8,128)(2,1)}, u32[]{:S(2)}, u32[]{:S(2)}) collective-permute-start(bf16[4,288,384]{2,1,0:T(8,128)(2,1)} %pad_maximum_fusion.2.refs_12_), channel_id=1, source_target_pairs={{0,16},{1,17},{2,18},{3,19},{4,20},{5,21},{6,22},{7,23},{8,24},{9,... | collective-permute-start | bytes 2654216 | tf_op jit(solution)/shard_map/ppermute | solution.py:423
  114.8 37.8 %collective-permute-start.11 = (bf16[4,288,240]{2,1,0:T(8,128)(2,1)}, bf16[4,288,240]{2,1,0:T(8,128)(2,1)S(1)}, u32[]{:S(2)}, u32[]{:S(2)}) collective-permute-start(bf16[4,288,240]{2,1,0:T(8,128)(2,1)} %copy-done.11), channel_id=1, source_target_pairs={{0,8},{1,9},{2,10},{3,11},{4,12},{5,13},{6,14},{7,15},{8,0},{9,1},... | collective-permute-start | bytes 1658888 | tf_op jit(solution)/shard_map/ppermute | solution.py:423
  128.4 36.1 %collective-permute-start.25 = (bf16[4,144,1056]{2,1,0:T(8,128)(2,1)}, bf16[4,144,1056]{2,1,0:T(8,128)(2,1)}, u32[]{:S(2)}, u32[]{:S(2)}) collective-permute-start(bf16[4,144,1056]{2,1,0:T(8,128)(2,1)} %pad_maximum_fusion.refs_0_), channel_id=1, source_target_pairs={{0,1},{1,0},{2,3},{3,2},{4,5},{5,4},{6,7},{7,6},{8,9},{9,8},{10,11... | collective-permute-start | bytes 3649544 | tf_op jit(solution)/shard_map/ppermute | solution.py:423
  133.6 47.4 %collective-permute-start.23 = (bf16[4,144,1056]{2,1,0:T(8,128)(2,1)}, bf16[4,144,1056]{2,1,0:T(8,128)(2,1)}, u32[]{:S(2)}, u32[]{:S(2)}) collective-permute-start(bf16[4,144,1056]{2,1,0:T(8,128)(2,1)} %pad_maximum_fusion.refs_0_), channel_id=1, source_target_pairs={{0,16},{1,17},{2,18},{3,19},{4,20},{5,21},{6,22},{7,23},{8,24},{9,... | collective-permute-start | bytes 3649544 | tf_op jit(solution)/shard_map/ppermute | solution.py:423
  135.2 45.8 %collective-permute-start.22 = (bf16[4,144,1056]{2,1,0:T(8,128)(2,1)}, bf16[4,144,1056]{2,1,0:T(8,128)(2,1)}, u32[]{:S(2)}, u32[]{:S(2)}) collective-permute-start(bf16[4,144,1056]{2,1,0:T(8,128)(2,1)} %pad_maximum_fusion.refs_0_), channel_id=1, source_target_pairs={{0,8},{1,9},{2,10},{3,11},{4,12},{5,13},{6,14},{7,15},{8,0},{9,1},... | collective-permute-start | bytes 3649544 | tf_op jit(solution)/shard_map/ppermute | solution.py:423
  152.6 28.9 %collective-permute-start.34 = (bf16[4,288,384]{2,1,0:T(8,128)(2,1)}, bf16[4,288,384]{2,1,0:T(8,128)(2,1)}, u32[]{:S(2)}, u32[]{:S(2)}) collective-permute-start(bf16[4,288,384]{2,1,0:T(8,128)(2,1)} %copy-done.23), channel_id=1, source_target_pairs={{0,8},{1,9},{2,10},{3,11},{4,12},{5,13},{6,14},{7,15},{8,0},{9,1},... | collective-permute-start | bytes 2654216 | tf_op jit(solution)/shard_map/ppermute | solution.py:423
  164.6 30.1 %collective-permute-start.50 = (bf16[4,288,384]{2,1,0:T(8,128)(2,1)}, bf16[4,288,384]{2,1,0:T(8,128)(2,1)}, u32[]{:S(2)}, u32[]{:S(2)}) collective-permute-start(bf16[4,288,384]{2,1,0:T(8,128)(2,1)} %collective-permute-done.48.refs_20_), channel_id=1, source_target_pairs={{0,16},{1,17},{2,18},{3,19},{4,20},{5,21},{6,22},{7,23},{8,24},{9,... | collective-permute-start | bytes 2654216 | tf_op jit(solution)/shard_map/ppermute | solution.py:423
  181.5 57.5 %collective-permute-start.27 = (bf16[4,144,1056]{2,1,0:T(8,128)(2,1)}, bf16[4,144,1056]{2,1,0:T(8,128)(2,1)}, u32[]{:S(2)}, u32[]{:S(2)}) collective-permute-start(bf16[4,144,1056]{2,1,0:T(8,128)(2,1)} %collective-permute-done.23.refs_2_), channel_id=1, source_target_pairs={{0,1},{1,0},{2,3},{3,2},{4,5},{5,4},{6,7},{7,6},{8,9},{9,8},{10,11... | collective-permute-start | bytes 3649544 | tf_op jit(solution)/shard_map/ppermute | solution.py:423
  196.5 34.1 %collective-permute-start.14 = (bf16[256,768]{1,0:T(8,128)(2,1)S(1)}, bf16[256,768]{1,0:T(8,128)(2,1)S(1)}, u32[]{:S(2)}, u32[]{:S(2)}) collective-permute-start(bf16[256,768]{1,0:T(8,128)(2,1)S(1)} %collective-permute-done.13.refs_2_), channel_id=1, source_target_pairs={{0,1},{1,0},{2,3},{3,2},{4,5},{5,4},{6,7},{7,6},{8,9},{9,8},{10,11... | collective-permute-start | bytes 1179656 | tf_op jit(solution)/shard_map/ppermute | solution.py:423
  196.8 42.1 %collective-permute-start.16 = (bf16[256,768]{1,0:T(8,128)(2,1)S(1)}, bf16[256,768]{1,0:T(8,128)(2,1)S(1)}, u32[]{:S(2)}, u32[]{:S(2)}) collective-permute-start(bf16[256,768]{1,0:T(8,128)(2,1)S(1)} %collective-permute-done.15.refs_4_), channel_id=1, source_target_pairs={{0,1},{1,0},{2,3},{3,2},{4,5},{5,4},{6,7},{7,6},{8,9},{9,8},{10,11... | collective-permute-start | bytes 1179656 | tf_op jit(solution)/shard_map/ppermute | solution.py:423
  206.7 39.9 %collective-permute-start.18 = (bf16[256,768]{1,0:T(8,128)(2,1)S(1)}, bf16[256,768]{1,0:T(8,128)(2,1)}, u32[]{:S(2)}, u32[]{:S(2)}) collective-permute-start(bf16[256,768]{1,0:T(8,128)(2,1)S(1)} %collective-permute-done.17.refs_6_), channel_id=1, source_target_pairs={{0,1},{1,0},{2,3},{3,2},{4,5},{5,4},{6,7},{7,6},{8,9},{9,8},{10,11... | collective-permute-start | bytes 1179656 | tf_op jit(solution)/shard_map/ppermute | solution.py:423
  222.1 46.8 %collective-permute-start.41 = (bf16[4,288,384]{2,1,0:T(8,128)(2,1)}, bf16[4,288,384]{2,1,0:T(8,128)(2,1)S(1)}, u32[]{:S(2)}, u32[]{:S(2)}) collective-permute-start(bf16[4,288,384]{2,1,0:T(8,128)(2,1)} %collective-permute-done.40.refs_14_), channel_id=1, source_target_pairs={{0,8},{1,9},{2,10},{3,11},{4,12},{5,13},{6,14},{7,15},{8,0},{9,1},... | collective-permute-start | bytes 2654216 | tf_op jit(solution)/shard_map/ppermute | solution.py:423
  230.5 38.4 %collective-permute-start.24 = (bf16[4,144,1056]{2,1,0:T(8,128)(2,1)}, bf16[4,144,1056]{2,1,0:T(8,128)(2,1)}, u32[]{:S(2)}, u32[]{:S(2)}) collective-permute-start(bf16[4,144,1056]{2,1,0:T(8,128)(2,1)} %collective-permute-done.23.refs_2_), channel_id=1, source_target_pairs={{0,8},{1,9},{2,10},{3,11},{4,12},{5,13},{6,14},{7,15},{8,0},{9,1},... | collective-permute-start | bytes 3649544 | tf_op jit(solution)/shard_map/ppermute | solution.py:423
  239.0 30.0 %collective-permute-start.26 = (bf16[4,144,1056]{2,1,0:T(8,128)(2,1)}, bf16[4,144,1056]{2,1,0:T(8,128)(2,1)}, u32[]{:S(2)}, u32[]{:S(2)}) collective-permute-start(bf16[4,144,1056]{2,1,0:T(8,128)(2,1)} %collective-permute-done.25.refs_4_), channel_id=1, source_target_pairs={{0,8},{1,9},{2,10},{3,11},{4,12},{5,13},{6,14},{7,15},{8,0},{9,1},... | collective-permute-start | bytes 3649544 | tf_op jit(solution)/shard_map/ppermute | solution.py:423
  239.0 30.0 %collective-permute-start.51 = (bf16[4,288,384]{2,1,0:T(8,128)(2,1)}, bf16[4,288,384]{2,1,0:T(8,128)(2,1)}, u32[]{:S(2)}, u32[]{:S(2)}) collective-permute-start(bf16[4,288,384]{2,1,0:T(8,128)(2,1)} %collective-permute-done.50.refs_22_), channel_id=1, source_target_pairs={{0,8},{1,9},{2,10},{3,11},{4,12},{5,13},{6,14},{7,15},{8,0},{9,1},... | collective-permute-start | bytes 2654216 | tf_op jit(solution)/shard_map/ppermute | solution.py:423
  404.5 52.4 %collective-permute-start.70 = (bf16[4,2,2,144,1056]{4,3,2,1,0:T(8,128)(2,1)}, bf16[4,2,2,144,1056]{4,3,2,1,0:T(8,128)(2,1)}, u32[]{:S(2)}, u32[]{:S(2)}) collective-permute-start(bf16[4,2,2,144,1056]{4,3,2,1,0:T(8,128)(2,1)} %get-tuple-element.67), channel_id=1, source_target_pairs={{0,8},{1,9},{2,10},{3,11},{4,12},{5,13},{6,14},{7,15},{8,0},{9,1},... | collective-permute-start | bytes 14598152 | tf_op jit(solution)/shard_map/ppermute | solution.py:423
  418.0 39.0 %collective-permute-start.71 = (bf16[4,2,2,288,384]{4,3,2,1,0:T(8,128)(2,1)}, bf16[4,2,2,288,384]{4,3,2,1,0:T(8,128)(2,1)}, u32[]{:S(2)}, u32[]{:S(2)}) collective-permute-start(bf16[4,2,2,288,384]{4,3,2,1,0:T(8,128)(2,1)} %get-tuple-element.68), channel_id=1, source_target_pairs={{0,8},{1,9},{2,10},{3,11},{4,12},{5,13},{6,14},{7,15},{8,0},{9,1},... | collective-permute-start | bytes 10616840 | tf_op jit(solution)/shard_map/ppermute | solution.py:423
  418.0 39.0 %collective-permute-start.72 = (bf16[4,2,2,288,384]{4,3,2,1,0:T(8,128)(2,1)}, bf16[4,2,2,288,384]{4,3,2,1,0:T(8,128)(2,1)}, u32[]{:S(2)}, u32[]{:S(2)}) collective-permute-start(bf16[4,2,2,288,384]{4,3,2,1,0:T(8,128)(2,1)} %get-tuple-element.69), channel_id=1, source_target_pairs={{0,8},{1,9},{2,10},{3,11},{4,12},{5,13},{6,14},{7,15},{8,0},{9,1},... | collective-permute-start | bytes 10616840 | tf_op jit(solution)/shard_map/ppermute | solution.py:423
  470.8 126.8 %collective-permute-start.73 = (bf16[4,2,144,1056]{3,2,1,0:T(8,128)(2,1)}, bf16[4,2,144,1056]{3,2,1,0:T(8,128)(2,1)}, u32[]{:S(2)}, u32[]{:S(2)}) collective-permute-start(bf16[4,2,144,1056]{3,2,1,0:T(8,128)(2,1)} %get-tuple-element.71), channel_id=1, source_target_pairs={{0,1},{1,0},{2,3},{3,2},{4,5},{5,4},{6,7},{7,6},{8,9},{9,8},{10,11... | collective-permute-start | bytes 7299080 | tf_op jit(solution)/shard_map/ppermute | solution.py:423
  472.7 116.7 %collective-permute-start.83 = (bf16[4,2,288,384]{3,2,1,0:T(8,128)(2,1)}, bf16[4,2,288,384]{3,2,1,0:T(8,128)(2,1)}, u32[]{:S(2)}, u32[]{:S(2)}) collective-permute-start(bf16[4,2,288,384]{3,2,1,0:T(8,128)(2,1)} %get-tuple-element.74), channel_id=1, source_target_pairs={{0,16},{1,17},{2,18},{3,19},{4,20},{5,21},{6,22},{7,23},{8,24},{9,... | collective-permute-start | bytes 5308424 | tf_op jit(solution)/shard_map/ppermute | solution.py:423
  474.2 119.3 %collective-permute-start.88 = (bf16[4,2,288,384]{3,2,1,0:T(8,128)(2,1)}, bf16[4,2,288,384]{3,2,1,0:T(8,128)(2,1)}, u32[]{:S(2)}, u32[]{:S(2)}) collective-permute-start(bf16[4,2,288,384]{3,2,1,0:T(8,128)(2,1)} %get-tuple-element.76), channel_id=1, source_target_pairs={{0,1},{1,0},{2,3},{3,2},{4,5},{5,4},{6,7},{7,6},{8,9},{9,8},{10,11... | collective-permute-start | bytes 5308424 | tf_op jit(solution)/shard_map/ppermute | solution.py:423
  486.6 101.9 %collective-permute-start.69 = (bf16[288,240]{1,0:T(8,128)(2,1)S(1)}, bf16[288,240]{1,0:T(8,128)(2,1)S(1)}, u32[]{:S(2)}, u32[]{:S(2)}) collective-permute-start(bf16[288,240]{1,0:T(8,128)(2,1)S(1)} %fusion.27), channel_id=1, source_target_pairs={{0,6},{1,7},{2,0},{3,1},{4,2},{5,3},{6,4},{7,5},{8,14},{9,15},{10,... | collective-permute-start | bytes 414728 | tf_op jit(solution)/shard_map/ppermute | solution.py:423
  516.2 51.8 %collective-permute-start.80 = (f32[1,1152]{1,0:T(1,128)S(1)}, f32[1,1152]{1,0:T(1,128)S(1)}, u32[]{:S(2)}, u32[]{:S(2)}) collective-permute-start(f32[1,1152]{1,0:T(1,128)S(1)} %add.224), channel_id=1, source_target_pairs={{0,1},{1,0},{2,3},{3,2},{4,5},{5,4},{6,7},{7,6},{8,9},{9,8},{10,11... | collective-permute-start | bytes 13832 | tf_op jit(solution)/shard_map/ppermute | solution.py:423
  600.3 38.4 %collective-permute-start.74 = (bf16[4,144,1056]{2,1,0:T(8,128)(2,1)}, bf16[4,144,1056]{2,1,0:T(8,128)(2,1)}, u32[]{:S(2)}, u32[]{:S(2)}) collective-permute-start(bf16[4,144,1056]{2,1,0:T(8,128)(2,1)} %fusion.4), channel_id=1, source_target_pairs={{0,16},{1,17},{2,18},{3,19},{4,20},{5,21},{6,22},{7,23},{8,24},{9,... | collective-permute-start | bytes 3649544 | tf_op jit(solution)/shard_map/ppermute | solution.py:423
  608.7 32.4 %collective-permute-start.85 = (bf16[288,384]{1,0:T(8,128)(2,1)S(1)}, bf16[288,384]{1,0:T(8,128)(2,1)S(1)}, u32[]{:S(2)}, u32[]{:S(2)}) collective-permute-start(bf16[288,384]{1,0:T(8,128)(2,1)S(1)} %slice_bitcast_fusion.15), channel_id=1, source_target_pairs={{0,6},{1,7},{2,0},{3,1},{4,2},{5,3},{6,4},{7,5},{8,14},{9,15},{10,... | collective-permute-start | bytes 663560 | tf_op jit(solution)/shard_map/ppermute | solution.py:423
  (92 other events, 1533.2 us)

commit v2 on v1

--- a/solution.py
+++ b/solution.py
@@ -17,7 +17,6 @@
 
 LANES = 128
 Z_SIZE = 4
-FLIPS = ((0, 0, 0), (0, 0, 1), (0, 1, 0), (0, 1, 1), (1, 0, 0), (1, 0, 1), (1, 1, 0), (1, 1, 1))
 VMEM_LIMIT = 66_000_000
 F32 = jnp.float32
 BF16 = jnp.bfloat16
@@ -423,22 +422,6 @@
     return lax.ppermute(array, ("seq", "ctx"), permute_pairs(axis, step))
 
 
-def gather_shards(shard, order):
-    held = {(0, 0, 0): shard}
-    for axis in order:
-        if axis == "z":
-            for place, array in list(held.items()):
-                ring = [array]
-                for _ in range(Z_SIZE - 1):
-                    ring.append(hop(ring[-1], "z", 1))
-                held[place] = jnp.stack(ring)
-        else:
-            at = ("x", "y", "core").index(axis)
-            for place, array in list(held.items()):
-                held[place[:at] + (1,) + place[at + 1 :]] = hop(array, axis)
-    return [held[flip] for flip in FLIPS]
-
-
 def add_pair(left, right):
     return (left.astype(F32) + right.astype(F32)).astype(BF16)
 
@@ -475,20 +458,6 @@
 
 def flipped(at, flip):
     return 1 - at if flip else at
-
-
-def block_copies(arrays, buffer, sems, column_major):
-    z, x, y, core = my_place()
-    copies = {}
-    for number, (dx, dy, dcore) in enumerate(FLIPS):
-        row, column = flipped(y, dy) * 2 + flipped(core, dcore), flipped(x, dx)
-        for t in range(Z_SIZE):
-            ctx_block = lax.rem(z - t + Z_SIZE, Z_SIZE) * 2 + column
-            target = buffer.at[ctx_block, row] if column_major else buffer.at[row, ctx_block]
-            copies[t, dx, dy, dcore] = pltpu.make_async_copy(
-                arrays[number].at[t], target, sems.at[number * Z_SIZE + t]
-            )
-    return copies
 
 
 def lane_ids(rows):
@@ -536,158 +505,386 @@
     return factor, rows * factor
 
 
-def project_kernel(tokens, gain, cosine, sine, *refs):
-    weights, (query_out, pair_out, buffer, pieces, wide, sems) = refs[:8], refs[8:]
-    z, x, _, _ = my_place()
-    copies = block_copies(weights, buffer, sems, True)
-    for copy in copies.values():
+def vmem_specs(count):
+    return [pl.BlockSpec(memory_space=pltpu.VMEM)] * count
+
+
+def any_specs(count):
+    return [pl.BlockSpec(memory_space=pl.ANY)] * count
+
+
+def cost(flops, moved, transcendentals=0):
+    return pl.CostEstimate(flops=int(flops), bytes_accessed=int(moved), transcendentals=int(transcendentals))
+
+
+def params():
+    return pltpu.CompilerParams(vmem_limit_bytes=VMEM_LIMIT)
+
+
+def masked_pair(block, half, other):
+    inside = (lane_ids(block.shape[0]) < HEAD_SIZE) == (half == 0)
+    return jnp.where(inside, block.astype(F32), other)
+
+
+class Gathering:
+    def __init__(self, own, full, block, sends, arrivals, corner_over_x):
+        self.own, self.full, self.block, self.sends, self.arrivals = own, full, block, sends, arrivals
+        self.corner_over_x = corner_over_x
+        self.started = []
+
+    def place(self, t, dx, dy, dcore=0):
+        z, x, y, core = my_place()
+        ctx_block = lax.rem(z - t + Z_SIZE, Z_SIZE) * 2 + flipped(x, dx)
+        return self.full.at[self.block(ctx_block, flipped(y, dy) * 2 + flipped(core, dcore))]
+
+    def copy(self, source, target, number, axis):
+        return pltpu.make_async_remote_copy(
+            src_ref=source,
+            dst_ref=target,
+            send_sem=self.sends.at[number],
+            recv_sem=self.arrivals.at[number],
+            device_id=neighbour(axis),
+            device_id_type=pl.DeviceIdType.MESH,
+        )
+
+    def send(self, piece, number, axis):
+        place = self.place(*piece)
+        copy = self.copy(self.own if piece == (0, 0, 0) else place, place, number, axis)
         copy.start()
+        self.started.append(copy)
+
+    def wait(self, piece, number, dcore=0):
+        place = self.place(*piece, dcore)
+        self.copy(place, place, number, "core").wait_recv()
+
+    def to_core(self, piece):
+        t, dx, dy = piece
+        self.send(piece, 15 + 4 * t + 2 * dx + dy, "core")
+
+    def over_z(self, t):
+        if t < Z_SIZE - 1:
+            self.send((t, 0, 0), t, "z")
+
+    def over_plane(self, t):
+        self.send((t, 0, 0), 3 + t, "x")
+        self.send((t, 0, 0), 7 + t, "y")
+
+    def begin(self):
+        self.over_z(0)
+        self.over_plane(0)
+        self.to_core((0, 0, 0))
+
+    def pass_on(self, t):
+        self.wait((t, 0, 0), t - 1)
+        self.over_z(t)
+        self.over_plane(t)
+        self.to_core((t, 0, 0))
+
+    def sides(self, t):
+        self.wait((t, 1, 0), 3 + t)
+        if t not in self.corner_over_x:
+            self.send((t, 1, 0), 11 + t, "y")
+        self.to_core((t, 1, 0))
+        self.wait((t, 0, 1), 7 + t)
+        if t in self.corner_over_x:
+            self.send((t, 0, 1), 11 + t, "x")
+        self.to_core((t, 0, 1))
+
+    def corner(self, t):
+        self.wait((t, 1, 1), 11 + t)
+        self.to_core((t, 1, 1))
+
+    def finish(self):
+        for t in range(Z_SIZE):
+            for dx in range(2):
+                for dy in range(2):
+                    self.wait((t, dx, dy), 15 + 4 * t + 2 * dx + dy, 1)
+
+    def drain(self):
+        for copy in self.started:
+            copy.wait_send()
+
+
+def neighbour(axis):
+    z, x, y, core = my_place()
+    if axis == "z":
+        z = lax.rem(z + 1, Z_SIZE)
+    elif axis == "z_back":
+        z = lax.rem(z + Z_SIZE - 1, Z_SIZE)
+    elif axis == "x":
+        x = 1 - x
+    elif axis == "y":
+        y = 1 - y
+    elif axis == "core":
+        core = 1 - core
+    elif axis == "y_core":
+        y, core = 1 - y, 1 - core
+    return (y * 2 + core, z * 2 + x)
+
+
+def meet(axes):
+    barrier = pltpu.get_barrier_semaphore()
+    for axis in axes:
+        pl.semaphore_signal(barrier, inc=1, device_id=neighbour(axis), device_id_type=pl.DeviceIdType.MESH)
+    pl.semaphore_wait(barrier, len(axes))
+
+
+def front_kernel(
+    qkv_own,
+    down_own,
+    up_own,
+    gains_own,
+    tokens,
+    cosine,
+    sine,
+    limit,
+    qkv,
+    down,
+    up,
+    pairs,
+    query_out,
+    attended,
+    log_total,
+    gain_out,
+    pieces,
+    wide,
+    keys,
+    values,
+    scores,
+    gains,
+    qkv_sends,
+    qkv_arrivals,
+    down_sends,
+    down_arrivals,
+    up_sends,
+    up_arrivals,
+    pair_sends,
+    pair_arrivals,
+    gain_sends,
+    gain_arrivals,
+    own_sems,
+):
+    z, x, y, core = my_place()
+    seq_at, ctx_at = y * 2 + core, z * 2 + x
+    by_ctx, by_seq = (lambda ctx, seq: (ctx, seq)), (lambda ctx, seq: (seq, ctx))
+    first = Gathering(qkv_own, qkv, by_ctx, qkv_sends, qkv_arrivals, (1, 3))
+    rest = (
+        Gathering(down_own, down, by_seq, down_sends, down_arrivals, (3,)),
+        Gathering(up_own, up, by_ctx, up_sends, up_arrivals, (3,)),
+    )
+    meet(("z", "z_back", "x", "y", "core", "y_core"))
+    first.begin()
+    gain_copies = []
+    for number, axis in enumerate(("core", "y", "y_core")):
+        copy = pltpu.make_async_remote_copy(
+            src_ref=gains_own,
+            dst_ref=gains.at[seq_at],
+            send_sem=gain_sends.at[number],
+            recv_sem=gain_arrivals.at[number],
+            device_id=neighbour(axis),
+            device_id_type=pl.DeviceIdType.MESH,
+        )
+        copy.start()
+        gain_copies.append(copy)
+    own_copies = [
+        pltpu.make_async_copy(source, target, own_sems.at[number])
+        for number, (source, target) in enumerate(
+            (
+                (qkv_own, first.place(0, 0, 0)),
+                (down_own, rest[0].place(0, 0, 0)),
+                (up_own, rest[1].place(0, 0, 0)),
+                (gains_own, gains.at[seq_at]),
+            )
+        )
+    ]
+    for copy in own_copies:
+        copy.start()
+    for t in range(1, Z_SIZE):
+        first.pass_on(t)
+        if t == Z_SIZE - 2:
+            for group in rest:
+                group.over_z(0)
+        first.sides(t - 1)
+    first.sides(Z_SIZE - 1)
+    for group in rest:
+        group.over_plane(0)
+        group.to_core((0, 0, 0))
+    for number, flips in enumerate(((0, 1), (1, 0), (1, 1))):
+        place = gains.at[flipped(y, flips[0]) * 2 + flipped(core, flips[1])]
+        pltpu.make_async_remote_copy(
+            src_ref=place,
+            dst_ref=place,
+            send_sem=gain_sends.at[number],
+            recv_sem=gain_arrivals.at[number],
+            device_id=neighbour("core"),
+            device_id_type=pl.DeviceIdType.MESH,
+        ).wait_recv()
+    for copy in own_copies:
+        copy.wait()
+    for row in range(4):
+        gain_out[:, row * 288 : (row + 1) * 288] = gains[row]
     _, hat = normalized(tokens[...].astype(F32))
-    rows = (hat * gain[...]).astype(BF16)
+    rows = (hat * gain_out[0:1, :]).astype(BF16)
     for t in range(Z_SIZE):
-        for dx in range(2):
-            for dy in range(2):
-                for dcore in range(2):
-                    copies[t, dx, dy, dcore].wait()
-            ctx_block = lax.rem(z - t + Z_SIZE, Z_SIZE) * 2 + flipped(x, dx)
-            matrix = buffer[ctx_block].reshape(tokens.shape[1], buffer.shape[3])
-            pieces[ctx_block] = jnp.dot(rows, matrix, preferred_element_type=F32)
+        first.corner(t)
+    first.finish()
+
+    def multiply(ctx_block, carry):
+        matrix = qkv[ctx_block].reshape(tokens.shape[1], 240)
+        pieces[ctx_block] = jnp.dot(rows, matrix, preferred_element_type=F32)
+        return carry
+
+    lax.fori_loop(0, 8, multiply, 0)
+    for group in rest:
+        group.pass_on(1)
     q_part, kv_part = 144, 48
     for at in range(8):
         wide[:, at * q_part : (at + 1) * q_part] = pieces[at, :, :q_part]
         wide[:, 1152 + at * kv_part : 1152 + (at + 1) * kv_part] = pieces[at, :, q_part : q_part + kv_part]
         wide[:, 1536 + at * kv_part : 1536 + (at + 1) * kv_part] = pieces[at, :, q_part + kv_part :]
     cos_tile, sin_tile = cosine[...], sine[...]
+    for pair in range(3):
+        key_tile = wide[:, 1152 + pair * LANES : 1152 + (pair + 1) * LANES]
+        pairs[ctx_at, :, 2 * pair * LANES : (2 * pair + 1) * LANES] = rotate_halves(
+            key_tile, cos_tile, sin_tile
+        ).astype(BF16)
+        pairs[ctx_at, :, (2 * pair + 1) * LANES : (2 * pair + 2) * LANES] = wide[
+            :, 1536 + pair * LANES : 1536 + (pair + 1) * LANES
+        ].astype(BF16)
     natural = [
         rotate_halves(wide[:, at * LANES : (at + 1) * LANES], cos_tile, sin_tile) * HEAD_SIZE**-0.5
         for at in range(9)
     ]
     for at, tile in enumerate(pair_tiles(natural)):
         query_out[at] = tile.astype(BF16)
-    for pair in range(3):
-        key_tile = wide[:, 1152 + pair * LANES : 1152 + (pair + 1) * LANES]
-        pair_out[:, 2 * pair * LANES : (2 * pair + 1) * LANES] = rotate_halves(
-            key_tile, cos_tile, sin_tile
-        ).astype(BF16)
-        pair_out[:, (2 * pair + 1) * LANES : (2 * pair + 2) * LANES] = wide[
-            :, 1536 + pair * LANES : 1536 + (pair + 1) * LANES
-        ].astype(BF16)
-
-
-def vmem_specs(count):
-    return [pl.BlockSpec(memory_space=pltpu.VMEM)] * count
-
-
-def any_specs(count):
-    return [pl.BlockSpec(memory_space=pl.ANY)] * count
-
-
-def cost(flops, moved, transcendentals=0):
-    return pl.CostEstimate(flops=int(flops), bytes_accessed=int(moved), transcendentals=int(transcendentals))
-
-
-def params():
-    return pltpu.CompilerParams(vmem_limit_bytes=VMEM_LIMIT)
-
-
-def project(tokens, gain, cosine, sine, weights):
-    rows, width = tokens.shape
-    _, shard_rows, shard_width = weights[0].shape
-    return pl.pallas_call(
-        project_kernel,
-        out_shape=(
-            jax.ShapeDtypeStruct((9, rows, LANES), BF16),
-            jax.ShapeDtypeStruct((rows, 768), BF16),
-        ),
-        in_specs=vmem_specs(4) + any_specs(8),
-        out_specs=tuple(vmem_specs(2)),
-        scratch_shapes=[
-            pltpu.VMEM((8, 4, shard_rows, shard_width), BF16),
-            pltpu.VMEM((8, rows, shard_width), F32),
-            pltpu.VMEM((rows, 1920), F32),
-            pltpu.SemaphoreType.DMA((32,)),
-        ],
-        compiler_params=params(),
-        cost_estimate=cost(2 * rows * width * 1920, 6e6),
-        name="project",
-    )(tokens, gain, cosine, sine, *weights)
-
-
-def slot_start(number):
-    z, x, _, _ = my_place()
-    return (lax.rem(z - number // 2 + Z_SIZE, Z_SIZE) * 2 + flipped(x, number % 2)) * 256
-
-
-def masked_pair(block, half, other):
-    inside = (lane_ids(block.shape[0]) < HEAD_SIZE) == (half == 0)
-    return jnp.where(inside, block.astype(F32), other)
-
-
-def attend_kernel(query, limit, *refs):
-    slots, (out, log_total, keys, values, scores) = refs[:8], refs[8:]
-
-    @pl.when(pl.program_id(1) == 0)
-    def _():
+
+    pair_copies = []
+
+    def pair_place(t, dx):
+        return pairs.at[lax.rem(z - t + Z_SIZE, Z_SIZE) * 2 + flipped(x, dx)]
+
+    def pair_copy(place, number, axis):
+        return pltpu.make_async_remote_copy(
+            src_ref=place,
+            dst_ref=place,
+            send_sem=pair_sends.at[number],
+            recv_sem=pair_arrivals.at[number],
+            device_id=neighbour(axis),
+            device_id_type=pl.DeviceIdType.MESH,
+        )
+
+    def pair_pass(t):
+        if t:
+            pair_copy(pair_place(t, 0), t - 1, "z").wait_recv()
+        for number, axis in ((t, "z"), (3 + t, "x")):
+            if axis == "x" or t < Z_SIZE - 1:
+                copy = pair_copy(pair_place(t, 0), number, axis)
+                copy.start()
+                pair_copies.append(copy)
+
+    def in_rest(step):
+        for group in rest:
+            step(group)
+
+    pair_pass(0)
+    pair_pass(1)
+    in_rest(lambda group: group.pass_on(2))
+    pair_pass(2)
+    in_rest(lambda group: group.sides(0))
+    pair_pass(3)
+    in_rest(lambda group: group.sides(1))
+    in_rest(lambda group: group.pass_on(3))
+    for t in range(Z_SIZE):
+        pair_copy(pair_place(t, 1), 3 + t, "x").wait_recv()
+
+    key_ids = lax.broadcasted_iota(jnp.int32, (256, tokens.shape[0]), 0)
+
+    def attend_pair(pair):
         for at in range(8):
             for half in range(2):
-                keys[half, at] = masked_pair(slots[at][:, :LANES], half, 0.0).astype(BF16)
-                values[half, at] = masked_pair(slots[at][:, LANES:], half, 1.0).T.astype(BF16)
-
-    rows = query.shape[1]
-    tile = query[0]
-    key_ids = lax.broadcasted_iota(jnp.int32, (256, rows), 0)
-    parts = []
-    for half in range(2):
-        top = None
-        for at in range(8):
-            part = lax.dot_general(keys[half, at], tile, NT, preferred_element_type=F32)
-            part = jnp.where(key_ids < limit[...] - slot_start(at), part, -1e30)
-            scores[at] = part
-            block_top = jnp.max(part, axis=0, keepdims=True)
-            top = block_top if top is None else jnp.maximum(top, block_top)
-        total = jnp.zeros((LANES, rows), F32)
-        for at in range(8):
-            weight = jnp.exp(scores[at] - top).astype(BF16)
-            total = total + jnp.dot(values[half, at], weight, preferred_element_type=F32)
-        norm = total[HEAD_SIZE : HEAD_SIZE + 1] if half == 0 else total[:1]
-        log_total[0, half : half + 1, :] = top + jnp.log(norm)
-        own = total[:HEAD_SIZE] if half == 0 else total[HEAD_SIZE:]
-        parts.append(own / norm)
-    out[0] = jnp.concatenate(parts, axis=0).T.astype(BF16)
-
-
-def attend(query, limit, slots):
-    rows = query.shape[1]
+                block = pairs[at, :, 2 * pair * LANES : (2 * pair + 1) * LANES]
+                keys[half, at] = masked_pair(block, half, 0.0).astype(BF16)
+                block = pairs[at, :, (2 * pair + 1) * LANES : (2 * pair + 2) * LANES]
+                values[half, at] = masked_pair(block, half, 1.0).T.astype(BF16)
+
+        def attend_member(member, carry):
+            tile = query_out[3 * pair + member]
+            parts = []
+            for half in range(2):
+                top = None
+                for at in range(8):
+                    part = lax.dot_general(keys[half, at], tile, NT, preferred_element_type=F32)
+                    part = jnp.where(key_ids < limit[...] - at * 256, part, -1e30)
+                    scores[at] = part
+                    block_top = jnp.max(part, axis=0, keepdims=True)
+                    top = block_top if top is None else jnp.maximum(top, block_top)
+                total = jnp.zeros((LANES, tile.shape[0]), F32)
+                for at in range(8):
+                    weight = jnp.exp(scores[at] - top).astype(BF16)
+                    total = total + jnp.dot(values[half, at], weight, preferred_element_type=F32)
+                norm = total[HEAD_SIZE : HEAD_SIZE + 1] if half == 0 else total[:1]
+                log_total[3 * pair + member, half : half + 1, :] = top + jnp.log(norm)
+                own = total[:HEAD_SIZE] if half == 0 else total[HEAD_SIZE:]
+                parts.append(own / norm)
+            attended[3 * pair + member] = jnp.concatenate(parts, axis=0).T.astype(BF16)
+            return carry
+
+        lax.fori_loop(0, 3, attend_member, 0)
+
+    attend_pair(0)
+    in_rest(lambda group: group.sides(2))
+    attend_pair(1)
+    in_rest(lambda group: group.sides(3))
+    attend_pair(2)
+    for t in range(Z_SIZE):
+        in_rest(lambda group: group.corner(t))
+    in_rest(lambda group: group.finish())
+    for group in (first,) + rest:
+        group.drain()
+    for copy in pair_copies + gain_copies:
+        copy.wait_send()
+
+
+def front(qkv_own, down_own, up_own, gains_own, tokens, cosine, sine, limit):
+    rows, width = tokens.shape
+    dma = pltpu.SemaphoreType.DMA
     return pl.pallas_call(
-        attend_kernel,
-        grid=(3, 3),
+        front_kernel,
         out_shape=(
+            jax.ShapeDtypeStruct((8, 4) + qkv_own.shape, BF16),
+            jax.ShapeDtypeStruct((4, 8) + down_own.shape, BF16),
+            jax.ShapeDtypeStruct((8, 4) + up_own.shape, BF16),
+            jax.ShapeDtypeStruct((8, rows, 768), BF16),
+            jax.ShapeDtypeStruct((9, rows, LANES), BF16),
             jax.ShapeDtypeStruct((9, rows, LANES), BF16),
             jax.ShapeDtypeStruct((9, 2, rows), F32),
+            jax.ShapeDtypeStruct((8, width), F32),
         ),
-        in_specs=[
-            pl.BlockSpec((1, rows, LANES), lambda p, g: (3 * p + g, 0, 0)),
-            pl.BlockSpec((1, rows), lambda p, g: (0, 0)),
-        ]
-        + [pl.BlockSpec((256, 2 * LANES), lambda p, g: (0, p))] * 8,
-        out_specs=(
-            pl.BlockSpec((1, rows, LANES), lambda p, g: (3 * p + g, 0, 0)),
-            pl.BlockSpec((1, 2, rows), lambda p, g: (3 * p + g, 0, 0)),
-        ),
+        in_specs=vmem_specs(1) + any_specs(2) + vmem_specs(5),
+        out_specs=tuple(vmem_specs(1) + any_specs(2) + vmem_specs(5)),
         scratch_shapes=[
+            pltpu.VMEM((8, rows, 240), F32),
+            pltpu.VMEM((rows, 1920), F32),
             pltpu.VMEM((2, 8, 256, LANES), BF16),
             pltpu.VMEM((2, 8, LANES, 256), BF16),
             pltpu.VMEM((8, 256, rows), F32),
-        ],
-        compiler_params=params(),
-        cost_estimate=cost(4 * 18 * rows * 2048 * 128 * 4, 6e6, 18 * rows * 2048),
-        name="attend",
-    )(query, limit, *slots)
+            pltpu.VMEM((4, 8, 288), F32),
+        ]
+        + [dma((31,))] * 6
+        + [dma((7,))] * 2
+        + [dma((3,))] * 2
+        + [dma((4,))],
+        compiler_params=pltpu.CompilerParams(
+            vmem_limit_bytes=VMEM_LIMIT, collective_id=1, has_side_effects=True
+        ),
+        cost_estimate=cost(4 * 18 * rows * 2048 * 128 * 4, 4e8, 18 * rows * 2048),
+        name="front",
+    )(qkv_own, down_own, up_own, gains_own, tokens, cosine, sine, limit)
 
 
 def attend_back_kernel(query, attended, grad, log_total, limit, cosine, sine, *refs):
-    slots, near, far = refs[:8], refs[8], refs[9:13]
-    query_grad, keys, keys_turned, values, key_sum, value_sum = refs[13:]
+    pairs, near, far = refs[0], refs[1], refs[2:6]
+    query_grad, keys, keys_turned, values, key_sum, value_sum = refs[6:]
 
     @pl.when(pl.program_id(1) == 0)
     def _():
@@ -695,10 +892,10 @@
         value_sum[...] = jnp.zeros_like(value_sum)
         for at in range(8):
             for half in range(2):
-                masked = masked_pair(slots[at][:, :LANES], half, 0.0)
+                masked = masked_pair(pairs[at, :, :LANES], half, 0.0)
                 keys[half, at] = masked.astype(BF16)
                 keys_turned[half, at] = masked.T.astype(BF16)
-                values[half, at] = masked_pair(slots[at][:, LANES:], half, 0.0).astype(BF16)
+                values[half, at] = masked_pair(pairs[at, :, LANES:], half, 0.0).astype(BF16)
 
     rows = query.shape[1]
     tile, grad_tile = query[0], grad[0]
@@ -713,7 +910,7 @@
         grad_half = masked_pair(grad_tile, half, 0.0).astype(BF16)
         for at in range(8):
             part = lax.dot_general(keys[half, at], tile, NT, preferred_element_type=F32)
-            part = jnp.where(key_ids < limit[...] - slot_start(at), part, -1e30)
+            part = jnp.where(key_ids < limit[...] - at * 256, part, -1e30)
             probs = jnp.exp(part - log_row)
             back = lax.dot_general(values[half, at], grad_tile, NT, preferred_element_type=F32)
             scored = (probs * (back - shift)).astype(BF16)
@@ -724,13 +921,15 @@
 
     @pl.when(pl.program_id(1) == 2)
     def _():
+        z, x, _, _ = my_place()
         for at in range(8):
+            block = lax.rem(z - at // 2 + Z_SIZE, Z_SIZE) * 2 + flipped(x, at % 2)
             ref = far[at // 2] if at % 2 else near.at[at // 2]
-            ref[:, :LANES] = key_sum[at].astype(BF16)
-            ref[:, LANES:] = value_sum[at].astype(BF16)
-
-
-def attend_back(query, attended, grad, log_total, limit, cosine, sine, slots):
+            ref[:, :LANES] = key_sum[block].astype(BF16)
+            ref[:, LANES:] = value_sum[block].astype(BF16)
+
+
+def attend_back(query, attended, grad, log_total, limit, cosine, sine, pairs):
     rows = query.shape[1]
     tile_spec = pl.BlockSpec((1, rows, LANES), lambda p, g: (3 * p + g, 0, 0))
     pair_spec = pl.BlockSpec((256, 2 * LANES), lambda p, g: (0, p))
@@ -750,7 +949,7 @@
             table_spec,
             table_spec,
         ]
-        + [pair_spec] * 8,
+        + [pl.BlockSpec((8, 256, 2 * LANES), lambda p, g: (0, 0, p))],
         out_specs=(pl.BlockSpec((4, 256, 2 * LANES), lambda p, g: (0, 0, p)),) + (pair_spec,) * 4 + (tile_spec,),
         scratch_shapes=[
             pltpu.VMEM((2, 8, 256, LANES), BF16),
@@ -762,24 +961,21 @@
         compiler_params=params(),
         cost_estimate=cost(4 * 18 * rows * 2048 * 128 * 10, 12e6, 18 * rows * 2048),
         name="attend_back",
-    )(query, attended, grad, log_total, limit, cosine, sine, *slots)
+    )(query, attended, grad, log_total, limit, cosine, sine, pairs)
 
 
 def middle_kernel(tokens, attended, cotangent, gain, *refs):
-    down_in, gate_in, up_in = refs[:8], refs[8:16], refs[16:24]
-    (output, hidden, gate_grad, up_grad, rows_two, mixed_grad, proj_grad, attended_out, attended_grad, gain_grad) = refs[24:34]
-    down, gate_w, up_w, gates, ups, wide, down_sems, gate_sems, up_sems = refs[34:]
-    z, x, _, _ = my_place()
-    down_copies = block_copies(down_in, down, down_sems, False)
-    gate_copies = block_copies(gate_in, gate_w, gate_sems, True)
-    up_copies = block_copies(up_in, up_w, up_sems, True)
-    for copies in (down_copies, gate_copies, up_copies):
-        for copy in copies.values():
-            copy.start()
+    down_in, up_in = refs[:2]
+    (output, hidden, gate_grad, up_grad, rows_two, mixed_grad, proj_grad, attended_out, attended_grad, gain_grad) = refs[2:12]
+    down, up_w, gates, ups, wide, down_sems, up_sems = refs[12:]
+    down_copies = [pltpu.make_async_copy(down_in.at[at], down.at[at], down_sems.at[at]) for at in range(4)]
+    up_copies = [pltpu.make_async_copy(up_in.at[at], up_w.at[at], up_sems.at[at]) for at in range(8)]
+    for copy in down_copies + up_copies:
+        copy.start()
     width = tokens.shape[1]
     for at, tile in enumerate(natural_tiles([attended[at].astype(F32) for at in range(9)])):
         wide[:, at * LANES : (at + 1) * LANES] = tile
-    for copy in down_copies.values():
+    for copy in down_copies:
         copy.wait()
 
     def out_block(row):
@@ -787,6 +983,12 @@
 
     def down_block(row):
         return down[row, :, :, :768].reshape(width, 768)
+
+    def gate_block(block):
+        return up_w[block, :, :, :384].reshape(width, 384)
+
+    def up_block(block):
+        return up_w[block, :, :, 384:].reshape(width, 384)
 
     mixed_grad[...] = tokens[...].astype(F32)
     for row in range(4):
@@ -797,15 +999,10 @@
     gains = gain[...]
     wide[...] = hat
     rows_two[...] = (hat * gains).astype(BF16)
-    for t in range(Z_SIZE):
-        for dx in range(2):
-            for dy in range(2):
-                for dcore in range(2):
-                    gate_copies[t, dx, dy, dcore].wait()
-                    up_copies[t, dx, dy, dcore].wait()
-            block = lax.rem(z - t + Z_SIZE, Z_SIZE) * 2 + flipped(x, dx)
-            gates[block] = jnp.dot(rows_two[...], gate_w[block].reshape(width, 384), preferred_element_type=F32)
-            ups[block] = jnp.dot(rows_two[...], up_w[block].reshape(width, 384), preferred_element_type=F32)
+    for block in range(8):
+        up_copies[block].wait()
+        gates[block] = jnp.dot(rows_two[...], gate_block(block), preferred_element_type=F32)
+        ups[block] = jnp.dot(rows_two[...], up_block(block), preferred_element_type=F32)
     for row in range(4):
         for side in range(2):
             gate, up = gates[2 * row + side], ups[2 * row + side]
@@ -822,10 +1019,10 @@
     output[...] = mixed_grad[...].astype(BF16)
     for block in range(8):
         grad_two = lax.dot_general(
-            gate_grad[block], gate_w[block].reshape(width, 384), NT, preferred_element_type=F32
+            gate_grad[block], gate_block(block), NT, preferred_element_type=F32
         )
         grad_two = grad_two + lax.dot_general(
-            up_grad[block], up_w[block].reshape(width, 384), NT, preferred_element_type=F32
+            up_grad[block], up_block(block), NT, preferred_element_type=F32
         )
         mixed_grad[...] = grad_two if block == 0 else mixed_grad[...] + grad_two
     grad_two, hat = mixed_grad[...], wide[...]
@@ -845,7 +1042,7 @@
         attended_grad[at] = tile.astype(BF16)
 
 
-def middle(tokens, attended, cotangent, gain, down, gate, up):
+def middle(tokens, attended, cotangent, gain, down, up):
     rows, width = tokens.shape
     return pl.pallas_call(
         middle_kernel,
@@ -861,23 +1058,21 @@
             jax.ShapeDtypeStruct((9, rows, LANES), BF16),
             jax.ShapeDtypeStruct((1, width), F32),
         ),
-        in_specs=vmem_specs(4) + any_specs(24),
+        in_specs=vmem_specs(4) + any_specs(2),
         out_specs=tuple(vmem_specs(10)),
         scratch_shapes=[
-            pltpu.VMEM((4, 8) + down[0].shape[1:], BF16),
-            pltpu.VMEM((8, 4) + gate[0].shape[1:], BF16),
-            pltpu.VMEM((8, 4) + up[0].shape[1:], BF16),
+            pltpu.VMEM(down.shape, BF16),
+            pltpu.VMEM(up.shape, BF16),
             pltpu.VMEM((8, rows, 384), F32),
             pltpu.VMEM((8, rows, 384), F32),
             pltpu.VMEM((rows, width), F32),
-            pltpu.SemaphoreType.DMA((32,)),
-            pltpu.SemaphoreType.DMA((32,)),
-            pltpu.SemaphoreType.DMA((32,)),
+            pltpu.SemaphoreType.DMA((4,)),
+            pltpu.SemaphoreType.DMA((8,)),
         ],
         compiler_params=params(),
         cost_estimate=cost(2 * rows * width * (6 * 3072 + 2 * 1152), 4e7),
         name="middle",
-    )(tokens, attended, cotangent, gain, *down, *gate, *up)
+    )(tokens, attended, cotangent, gain, down, up)
 
 
 def turned_rows(matrix, parts):
@@ -961,12 +1156,10 @@
 
 
 def project_back_kernel(tokens, gain, query_grad, pair_grad, mixed_grad, cosine, sine, *refs):
-    weights = refs[:8]
-    input_grad, gain_grad, send, kept, buffer, pieces, wide, rows_turned, sems = refs[8:]
+    weights, input_grad, gain_grad, send, kept, buffer, pieces, wide, rows_turned, sem = refs
     z, x, y, core = my_place()
-    copies = block_copies(weights, buffer, sems, True)
-    for copy in copies.values():
-        copy.start()
+    copy = pltpu.make_async_copy(weights, buffer, sem)
+    copy.start()
     width = tokens.shape[1]
     factor, hat = normalized(tokens[...].astype(F32))
     gains = gain[...]
@@ -998,8 +1191,7 @@
                     row = flipped(y, dy) * 2 + (core if keep else 1 - core)
                     value = jnp.dot(rows_turned[row], pieces[block], preferred_element_type=F32)
                     (kept if keep else send)[t, dx, dy] = value.astype(BF16)
-    for copy in copies.values():
-        copy.wait()
+    copy.wait()
     grad_one = jnp.zeros_like(hat)
     for block in range(8):
         grad_one = grad_one + lax.dot_general(
@@ -1014,7 +1206,7 @@
 
 def project_back(tokens, gain, query_grad, pair_grad, mixed_grad, cosine, sine, weights):
     rows, width = tokens.shape
-    piece = weights[0].shape[1:]
+    piece = weights.shape[2:]
     return pl.pallas_call(
         project_back_kernel,
         out_shape=(
@@ -1023,19 +1215,19 @@
             jax.ShapeDtypeStruct((Z_SIZE, 2, 2) + piece, BF16),
             jax.ShapeDtypeStruct((Z_SIZE, 2, 2) + piece, BF16),
         ),
-        in_specs=vmem_specs(7) + any_specs(8),
+        in_specs=vmem_specs(7) + any_specs(1),
         out_specs=tuple(vmem_specs(4)),
         scratch_shapes=[
             pltpu.VMEM((8, 4) + piece, BF16),
             pltpu.VMEM((8, rows, 240), BF16),
             pltpu.VMEM((rows, 1920), F32),
             pltpu.VMEM((4, 288, rows), BF16),
-            pltpu.SemaphoreType.DMA((32,)),
+            pltpu.SemaphoreType.DMA,
         ],
         compiler_params=params(),
         cost_estimate=cost(4 * rows * width * 1920, 1.4e7),
         name="project_back",
-    )(tokens, gain, query_grad, pair_grad, mixed_grad, cosine, sine, *weights)
+    )(tokens, gain, query_grad, pair_grad, mixed_grad, cosine, sine, weights)
 
 
 def lane_tables(first, rows):
@@ -1046,36 +1238,26 @@
     return jnp.tile(cosine, (1, 4)), jnp.tile(jnp.concatenate([-sine, sine], axis=1), (1, 2))
 
 
-def gather_gains(gain_one, gain_two):
-    held = jnp.stack([gain_one, gain_two])
-    near = jnp.stack([held, hop(held, "core")])
-    every = jnp.concatenate([near, hop(near, "y")])
-    order = jnp.arange(4) ^ lax.axis_index("seq")
-    every = jnp.take(every, order, axis=0).astype(F32)
-    return every[:, 0].reshape(1, -1), every[:, 1].reshape(1, -1)
-
-
 def permuted_device(
     tokens, prefix, gain_one, w_query, w_key, value_weight, w_out, gain_two, w_gate, w_up, w_down, cotangent
 ):
     _, rows, width = tokens.shape
     tokens, cotangent = tokens[0], cotangent[0]
     ctx_at, seq_at = lax.axis_index("ctx"), lax.axis_index("seq")
-    first_norm, second_norm = gather_gains(gain_one, gain_two)
-    qkv = gather_shards(jnp.concatenate([w_query, w_key, value_weight], axis=1), ("z", "x", "y", "core"))
-    down = gather_shards(jnp.concatenate([w_down.T, w_out.T], axis=1), ("z", "y", "x", "core"))
-    gate = gather_shards(w_gate, ("x", "z", "y", "core"))
-    up = gather_shards(w_up, ("z", "x", "y", "core"))
+    gains = jnp.zeros((8, gain_one.shape[0]), F32).at[0].set(gain_one.astype(F32)).at[1].set(gain_two.astype(F32))
     cosine, sine = lane_tables(ctx_at * rows, rows)
     limit = jnp.maximum(ctx_at * rows + jnp.arange(rows, dtype=jnp.int32) + 1, prefix[0])[None, :]
-
-    query, pair = project(tokens, first_norm, cosine, sine, qkv)
-    slots, held = [], pair
-    for t in range(Z_SIZE):
-        slots += [held, hop(held, "x")]
-        if t < Z_SIZE - 1:
-            held = hop(held, "z", 1)
-    attended, log_total = attend(query, limit, slots)
+    qkv, down, up, pairs, query, attended, log_total, gains = front(
+        jnp.concatenate([w_query, w_key, value_weight], axis=1),
+        jnp.concatenate([w_down.T, w_out.T], axis=1),
+        jnp.concatenate([w_gate, w_up], axis=1),
+        gains,
+        tokens,
+        cosine,
+        sine,
+        limit,
+    )
+    first_norm, second_norm = gains[0:1], gains[1:2]
     (
         output,
         hidden,
@@ -1087,21 +1269,23 @@
         attended_rows,
         attended_grad,
         second_gain_part,
-    ) = middle(tokens, attended, cotangent, second_norm, down, gate, up)
+    ) = middle(tokens, attended, cotangent, second_norm, down, up)
 
     first = ("x", "y", "x")
     factors = (rows_two, gate_grad, up_grad, hidden, cotangent, proj_grad, attended_rows)
     sent = weight_grads(False, first, *factors)
+    attended_grad, sent = lax.optimization_barrier((attended_grad, sent))
     arrived = [hop(array, "core") for array in sent]
+    near, *far, query_grad = attend_back(
+        query, attended, attended_grad, log_total, limit, cosine, sine, pairs
+    )
+    arrived, near, far = lax.optimization_barrier((arrived, near, far))
     parts = weight_grads(True, first, *factors, arrived)
     grad_down_out, grad_gate, grad_up = [
         scatter_rest(parts[at], parts[3 + at], first[at]) for at in range(3)
     ]
     second_gain_gradient = sum_everywhere(second_gain_part)
 
-    near, *far, query_grad = attend_back(
-        query, attended, attended_grad, log_total, limit, cosine, sine, slots
-    )
     total = add_pair(near[3], hop(far[3], "x"))
     for t in (2, 1, 0):
         local = near[t].astype(F32) + hop(far[t], "x").astype(F32)

time: 685 us -> 565 us (0.82)
  waiting for transfers between devices: 394 us -> 196 us
  Pallas kernels: 150 us -> 278 us
  starting transfers between devices: 83.4 us -> 45 us
  other arithmetic: 33.6 us -> 23.1 us
    ppermute x93 -> x41, waiting for transfers between devices: 394 us -> 196 us  [hop(): return lax.ppermute(array, ('seq', 'ctx'), permute_pairs(axis, step))]
    pallas_call x2 -> x1, Pallas kernels: 32.2 us -> 161 us  [front(): pl.pallas_call(front_kernel, out_shape=(jax.ShapeDtypeStruct((8, 4) + qkv...]
    ppermute x93 -> x41, starting transfers between devices: 83.4 us -> 45 us  [hop(): return lax.ppermute(array, ('seq', 'ctx'), permute_pairs(axis, step))]
  transfers between devices with their start and end apart: 93 -> 41, of which waited for: 52 -> 23; matrix products, arithmetic and copies ran while one was open for 6% -> 4% of each run, Pallas kernels for 10% -> 12%
where the time goes in v2:
time: 565 us; the launch traced here: 557 us
  Pallas kernels  278 us (49%)
  waiting for transfers between devices  196 us (35%)
  starting transfers between devices  45 us (8%)
  other arithmetic  23.1 us (4%)
  local copies, waits for them, and re-layouts  12 us (2%)
    ppermute x41, waiting for transfers between devices, hop(): return lax.ppermute(array, ('seq', 'ctx'), permute_pairs(axis, step))  196 us
    pallas_call x1, Pallas kernels, front(): pl.pallas_call(front_kernel, out_shape=(jax.ShapeDtypeStruct((8, 4) + qkv...  161 us
    ppermute x41, starting transfers between devices, hop(): return lax.ppermute(array, ('seq', 'ctx'), permute_pairs(axis, step))  45 us
    pallas_call x1, Pallas kernels, attend_back(): pl.pallas_call(attend_back_kernel, grid=(3, 3), out_shape=(jax.ShapeDtype...  41.7 us
    pallas_call x1, Pallas kernels, middle(): pl.pallas_call(middle_kernel, out_shape=(jax.ShapeDtypeStruct((rows, widt...  41.6 us
    pallas_call x2, Pallas kernels, weight_grads(): pl.pallas_call(functools.partial(weight_grad_kernel, keep, first), grid=(...  24.1 us
    convert_element_type x18, other arithmetic, add_pair(): return (left.astype(F32) + right.astype(F32)).astype(BF16)  13.1 us
  transfers between devices with their start and end apart: 41, of which 23 were waited for; matrix products, arithmetic and copies ran while one was open for 4% of the time, Pallas kernels for 12%

profile of v2, /device:TPU:0, one launch (start us, length us, event | category | flops | bytes accessed | tf_op | source)
XLA Modules:
  0.0 556.5 jit_solution(8376500168027028762)
XLA Ops:
  11.8 161.3 %front.1 = (bf16[8,4,288,240]{3,2,1,0:T(8,128)(2,1)}, bf16[4,8,144,1056]{3,2,1,0:T(8,128)(2,1)}, bf16[8,4,288,768]{3,2,1,0:T(8,128)(2,1)}, bf16[8,256,768]{2,1,0...) custom-call(bf16[288,240]{1,0:T(8,128)(2,1)} %pad_maximum_fusion.2.q, ...), custom_call_target="tpu_custom_call" | custom-call | flops 19327352832 | bytes 400000000 | tf_op jit(solution)/shard_map/front/pallas_call | solution.py:851
  174.5 41.6 %middle.1 = (bf16[256,1152]{1,0:T(8,128)(2,1)}, bf16[4,256,768]{2,1,0:T(8,128)(2,1)}, bf16[8,256,384]{2,1,0:T(8,128)(2,1)}, bf16[8,256,384]{2,1,0:T(8,128)(2,1)}...) custom-call(bf16[256,1152]{1,0:T(8,128)(2,1)} %bitcast.160, ...), custom_call_target="tpu_custom_call" | custom-call | flops 12230590464 | bytes 40000000 | tf_op jit(solution)/shard_map/middle/pallas_call | solution.py:1047
  216.2 10.3 %weight_grads_send.1 = (bf16[4,2,2,144,1056]{4,3,2,1,0:T(8,128)(2,1)}, bf16[4,2,2,288,384]{4,3,2,1,0:T(8,128)(2,1)}, bf16[4,2,2,288,384]{4,3,2,1,0:T(8,128)(2,1)}) custom-call(bf16[256,1152]{1,0:T(8,128)(2,1)} %get-tuple-element.91.rows_two, bf16[8,256,384]{2,1,0:T(8,128)(2,1)} %get-tuple-element.92.gate_grad, ...), custom_call_target="tpu_custom_call" | custom-call | flops 3057647616 | bytes 30000000 | tf_op jit(solution)/shard_map/weight_grads_send/pallas_call | solution.py:1138
  227.5 41.7 %attend_back.1 = (bf16[4,256,768]{2,1,0:T(8,128)(2,1)}, bf16[256,768]{1,0:T(8,128)(2,1)}, bf16[256,768]{1,0:T(8,128)(2,1)}, bf16[256,768]{1,0:T(8,128)(2,1)}, bf...) custom-call(bf16[9,256,128]{2,1,0:T(8,128)(2,1)} %get-tuple-element.89.query, ...), custom_call_target="tpu_custom_call" | custom-call | flops 48318382080 | bytes 12000000 | tf_op jit(solution)/shard_map/attend_back/pallas_call | solution.py:937
  271.3 10.2 %collective-permute-done.6 = bf16[256,768]{1,0:T(8,128)(2,1)S(1)} collective-permute-done((bf16[256,768]{1,0:T(8,128)(2,1)}, bf16[256,768]{1,0:T(8,128)(2,1)S(1)}, u32[]{:S(2)}, u32[]{:S(2)}) %collective-permute-start.6) | collective-permute-done | bytes 393248 | tf_op jit(solution)/shard_map/ppermute | solution.py:422
  281.5 1.8 fusion.11
  283.6 13.8 %weight_grads_keep.1 = (bf16[4,2,144,1056]{3,2,1,0:T(8,128)(2,1)}, bf16[4,2,288,384]{3,2,1,0:T(8,128)(2,1)}, bf16[4,2,288,384]{3,2,1,0:T(8,128)(2,1)}, bf16[4,2,...) custom-call(bf16[256,1152]{1,0:T(8,128)(2,1)} %get-tuple-element.91.rows_two, ...), custom_call_target="tpu_custom_call" | custom-call | flops 3057647616 | bytes 30000000 | tf_op jit(solution)/shard_map/weight_grads_keep/pallas_call | solution.py:1138
  297.4 2.2 collective-permute-start.21
  303.5 63.2 %collective-permute-done.4 = bf16[256,768]{1,0:T(8,128)(2,1)S(1)} collective-permute-done((bf16[256,768]{1,0:T(8,128)(2,1)}, bf16[256,768]{1,0:T(8,128)(2,1)S(1)}, u32[]{:S(2)}, u32[]{:S(2)}) %collective-permute-start.4) | collective-permute-done | bytes 393248 | tf_op jit(solution)/shard_map/ppermute | solution.py:422
  366.7 2.0 collective-permute-start.3
  369.1 41.5 %collective-permute-done.3 = bf16[256,768]{1,0:T(8,128)(2,1)S(1)} collective-permute-done((bf16[256,768]{1,0:T(8,128)(2,1)}, bf16[256,768]{1,0:T(8,128)(2,1)S(1)}, u32[]{:S(2)}, u32[]{:S(2)}) %collective-permute-start.3) | collective-permute-done | bytes 393248 | tf_op jit(solution)/shard_map/ppermute | solution.py:422
  411.5 9.8 %project_back.1 = (f32[256,1152]{1,0:T(8,128)}, f32[1,1152]{1,0:T(1,128)}, bf16[4,2,2,288,240]{4,3,2,1,0:T(8,128)(2,1)}, bf16[4,2,2,288,240]{4,3,2,1,0:T(8,128)(2,1)}) custom-call(bf16[256,1152]{1,0:T(8,128)(2,1)} %bitcast.161, f32[1,1152]{1,0:T(1,128)} %get-tuple-element.159.gain, bf16[9,256,128]{2,1,0:T(8,128)(2,1)} %get-tuple-element.103.query_grad, ...), custom_call_target="tpu_custom_call" | custom-call | flops 2264924160 | bytes 14000000 | tf_op jit(solution)/shard_map/project_back/pallas_call | solution.py:1210
  432.9 1.8 collective-permute-done.13
  445.4 1.8 fusion.4
  448.2 14.3 %collective-permute-done.32 = bf16[4,288,384]{2,1,0:T(8,128)(2,1)S(1)} collective-permute-done((bf16[4,288,384]{2,1,0:T(8,128)(2,1)S(1)}, bf16[4,288,384]{2,1,0:T(8,128)(2,1)S(1)}, u32[]{:S(2)}, u32[]{:S(2)}) %collective-permute-start.32) | collective-permute-done | bytes 884768 | tf_op jit(solution)/shard_map/ppermute | solution.py:422
  465.0 1.9 collective-permute-done.37
  470.2 2.2 collective-permute-done.33
  472.5 2.6 collective-permute-start.34
  475.1 2.1 collective-permute-done.38
  477.2 2.7 collective-permute-start.39
  479.9 2.0 collective-permute-done.34
  482.0 3.4 collective-permute-start.35
  485.4 8.2 %collective-permute-done.22 = bf16[4,144,1056]{2,1,0:T(8,128)(2,1)S(1)} collective-permute-done((bf16[4,144,1056]{2,1,0:T(8,128)(2,1)S(1)}, bf16[4,144,1056]{2,1,0:T(8,128)(2,1)S(1)}, u32[]{:S(2)}, u32[]{:S(2)}) %collective-permute-start.22) | collective-permute-done | bytes 1216544 | tf_op jit(solution)/shard_map/ppermute | solution.py:422
  493.6 1.8 fusion
  500.1 7.5 %collective-permute-done.23 = bf16[144,1056]{1,0:T(8,128)(2,1)S(1)} collective-permute-done((bf16[144,1056]{1,0:T(8,128)(2,1)S(1)}, bf16[144,1056]{1,0:T(8,128)(2,1)S(1)}, u32[]{:S(2)}, u32[]{:S(2)}) %collective-permute-start.23) | collective-permute-done | bytes 304160 | tf_op jit(solution)/shard_map/ppermute | solution.py:422
  507.7 2.9 collective-permute-start.24
  510.7 11.9 %collective-permute-done.16 = bf16[4,2,288,240]{3,2,1,0:T(8,128)(2,1)S(1)} collective-permute-done((bf16[4,2,288,240]{3,2,1,0:T(8,128)(2,1)S(1)}, bf16[4,2,288,240]{3,2,1,0:T(8,128)(2,1)S(1)}, u32[]{:S(2)}, u32[]{:S(2)}) %collective-permute-start.16) | collective-permute-done | bytes 1105952 | tf_op jit(solution)/shard_map/ppermute | solution.py:422
  524.5 10.9 %collective-permute-done.17 = bf16[4,288,240]{2,1,0:T(8,128)(2,1)S(1)} collective-permute-done((bf16[4,288,240]{2,1,0:T(8,128)(2,1)S(1)}, bf16[4,288,240]{2,1,0:T(8,128)(2,1)S(1)}, u32[]{:S(2)}, u32[]{:S(2)}) %collective-permute-start.17) | collective-permute-done | bytes 552992 | tf_op jit(solution)/shard_map/ppermute | solution.py:422
  535.9 6.2 %collective-permute-done.18 = bf16[288,240]{1,0:T(8,128)(2,1)S(1)} collective-permute-done((bf16[288,240]{1,0:T(8,128)(2,1)S(1)}, bf16[288,240]{1,0:T(8,128)(2,1)S(1)}, u32[]{:S(2)}, u32[]{:S(2)}) %collective-permute-start.18) | collective-permute-done | bytes 138272 | tf_op jit(solution)/shard_map/ppermute | solution.py:422
  543.6 4.2 collective-permute-done.19
  547.8 3.2 collective-permute-start.20
  551.7 2.0 collective-permute-done.20
  (143 shorter events, 61.4 us)
Async XLA Ops:
  226.5 42.7 %collective-permute-start = (bf16[4,2,2,144,1056]{4,3,2,1,0:T(8,128)(2,1)}, bf16[4,2,2,144,1056]{4,3,2,1,0:T(8,128)(2,1)}, u32[]{:S(2)}, u32[]{:S(2)}) collective-permute-start(bf16[4,2,2,144,1056]{4,3,2,1,0:T(8,128)(2,1)} %get-tuple-element.104), channel_id=1, source_target_pairs={{0,8},{1,9},{2,10},{3,11},{4,12},{5,13},{6,14},{7,15},{8,0},{9,1},... | collective-permute-start | bytes 14598152 | tf_op jit(solution)/shard_map/ppermute | solution.py:422
  227.0 42.2 %collective-permute-start.1 = (bf16[4,2,2,288,384]{4,3,2,1,0:T(8,128)(2,1)}, bf16[4,2,2,288,384]{4,3,2,1,0:T(8,128)(2,1)}, u32[]{:S(2)}, u32[]{:S(2)}) collective-permute-start(bf16[4,2,2,288,384]{4,3,2,1,0:T(8,128)(2,1)} %get-tuple-element.105), channel_id=1, source_target_pairs={{0,8},{1,9},{2,10},{3,11},{4,12},{5,13},{6,14},{7,15},{8,0},{9,1},... | collective-permute-start | bytes 10616840 | tf_op jit(solution)/shard_map/ppermute | solution.py:422
  227.1 42.1 %collective-permute-start.2 = (bf16[4,2,2,288,384]{4,3,2,1,0:T(8,128)(2,1)}, bf16[4,2,2,288,384]{4,3,2,1,0:T(8,128)(2,1)}, u32[]{:S(2)}, u32[]{:S(2)}) collective-permute-start(bf16[4,2,2,288,384]{4,3,2,1,0:T(8,128)(2,1)} %get-tuple-element.106), channel_id=1, source_target_pairs={{0,8},{1,9},{2,10},{3,11},{4,12},{5,13},{6,14},{7,15},{8,0},{9,1},... | collective-permute-start | bytes 10616840 | tf_op jit(solution)/shard_map/ppermute | solution.py:422
  269.2 12.2 %collective-permute-start.6 = (bf16[256,768]{1,0:T(8,128)(2,1)}, bf16[256,768]{1,0:T(8,128)(2,1)S(1)}, u32[]{:S(2)}, u32[]{:S(2)}) collective-permute-start(bf16[256,768]{1,0:T(8,128)(2,1)} %get-tuple-element.116), channel_id=1, source_target_pairs={{0,1},{1,0},{2,3},{3,2},{4,5},{5,4},{6,7},{7,6},{8,9},{9,8},{10,11... | collective-permute-start | bytes 1179656 | tf_op jit(solution)/shard_map/ppermute | solution.py:422
  270.5 30.7 %collective-permute-start.5 = (bf16[256,768]{1,0:T(8,128)(2,1)}, bf16[256,768]{1,0:T(8,128)(2,1)S(1)}, u32[]{:S(2)}, u32[]{:S(2)}) collective-permute-start(bf16[256,768]{1,0:T(8,128)(2,1)} %get-tuple-element.115), channel_id=1, source_target_pairs={{0,1},{1,0},{2,3},{3,2},{4,5},{5,4},{6,7},{7,6},{8,9},{9,8},{10,11... | collective-permute-start | bytes 1179656 | tf_op jit(solution)/shard_map/ppermute | solution.py:422
  283.3 17.9 %collective-permute-start.7 = (bf16[256,768]{1,0:T(8,128)(2,1)}, bf16[256,768]{1,0:T(8,128)(2,1)S(1)}, u32[]{:S(2)}, u32[]{:S(2)}) collective-permute-start(bf16[256,768]{1,0:T(8,128)(2,1)} %fusion.11), channel_id=1, source_target_pairs={{0,6},{1,7},{2,0},{3,1},{4,2},{5,3},{6,4},{7,5},{8,14},{9,15},{10,... | collective-permute-start | bytes 1179656 | tf_op jit(solution)/shard_map/ppermute | solution.py:422
  297.4 148.0 %collective-permute-start.21 = (bf16[4,2,144,1056]{3,2,1,0:T(8,128)(2,1)}, bf16[4,2,144,1056]{3,2,1,0:T(8,128)(2,1)}, u32[]{:S(2)}, u32[]{:S(2)}) collective-permute-start(bf16[4,2,144,1056]{3,2,1,0:T(8,128)(2,1)} %get-tuple-element.127), channel_id=1, source_target_pairs={{0,1},{1,0},{2,3},{3,2},{4,5},{5,4},{6,7},{7,6},{8,9},{9,8},{10,11... | collective-permute-start | bytes 7299080 | tf_op jit(solution)/shard_map/ppermute | solution.py:422
  299.5 67.1 %collective-permute-start.4 = (bf16[256,768]{1,0:T(8,128)(2,1)}, bf16[256,768]{1,0:T(8,128)(2,1)S(1)}, u32[]{:S(2)}, u32[]{:S(2)}) collective-permute-start(bf16[256,768]{1,0:T(8,128)(2,1)} %get-tuple-element.114), channel_id=1, source_target_pairs={{0,1},{1,0},{2,3},{3,2},{4,5},{5,4},{6,7},{7,6},{8,9},{9,8},{10,11... | collective-permute-start | bytes 1179656 | tf_op jit(solution)/shard_map/ppermute | solution.py:422
  299.6 140.2 %collective-permute-start.31 = (bf16[4,2,288,384]{3,2,1,0:T(8,128)(2,1)}, bf16[4,2,288,384]{3,2,1,0:T(8,128)(2,1)}, u32[]{:S(2)}, u32[]{:S(2)}) collective-permute-start(bf16[4,2,288,384]{3,2,1,0:T(8,128)(2,1)} %get-tuple-element.130), channel_id=1, source_target_pairs={{0,16},{1,17},{2,18},{3,19},{4,20},{5,21},{6,22},{7,23},{8,24},{9,... | collective-permute-start | bytes 5308424 | tf_op jit(solution)/shard_map/ppermute | solution.py:422
  302.4 66.3 %collective-permute-start.8 = (bf16[256,768]{1,0:T(8,128)(2,1)S(1)}, bf16[256,768]{1,0:T(8,128)(2,1)S(1)}, u32[]{:S(2)}, u32[]{:S(2)}) collective-permute-start(bf16[256,768]{1,0:T(8,128)(2,1)S(1)} %fusion.13), channel_id=1, source_target_pairs={{0,6},{1,7},{2,0},{3,1},{4,2},{5,3},{6,4},{7,5},{8,14},{9,15},{10,... | collective-permute-start | bytes 1179656 | tf_op jit(solution)/shard_map/ppermute | solution.py:422
  302.4 140.5 %collective-permute-start.36 = (bf16[4,2,288,384]{3,2,1,0:T(8,128)(2,1)}, bf16[4,2,288,384]{3,2,1,0:T(8,128)(2,1)}, u32[]{:S(2)}, u32[]{:S(2)}) collective-permute-start(bf16[4,2,288,384]{3,2,1,0:T(8,128)(2,1)} %get-tuple-element.132), channel_id=1, source_target_pairs={{0,1},{1,0},{2,3},{3,2},{4,5},{5,4},{6,7},{7,6},{8,9},{9,8},{10,11... | collective-permute-start | bytes 5308424 | tf_op jit(solution)/shard_map/ppermute | solution.py:422
  366.7 43.9 %collective-permute-start.3 = (bf16[256,768]{1,0:T(8,128)(2,1)}, bf16[256,768]{1,0:T(8,128)(2,1)S(1)}, u32[]{:S(2)}, u32[]{:S(2)}) collective-permute-start(bf16[256,768]{1,0:T(8,128)(2,1)} %get-tuple-element.113), channel_id=1, source_target_pairs={{0,1},{1,0},{2,3},{3,2},{4,5},{5,4},{6,7},{7,6},{8,9},{9,8},{10,11... | collective-permute-start | bytes 1179656 | tf_op jit(solution)/shard_map/ppermute | solution.py:422
  368.8 41.8 %collective-permute-start.9 = (bf16[256,768]{1,0:T(8,128)(2,1)S(1)}, bf16[256,768]{1,0:T(8,128)(2,1)S(1)}, u32[]{:S(2)}, u32[]{:S(2)}) collective-permute-start(bf16[256,768]{1,0:T(8,128)(2,1)S(1)} %fusion.15), channel_id=1, source_target_pairs={{0,6},{1,7},{2,0},{3,1},{4,2},{5,3},{6,4},{7,5},{8,14},{9,15},{10,... | collective-permute-start | bytes 1179656 | tf_op jit(solution)/shard_map/ppermute | solution.py:422
  410.6 11.3 %collective-permute-start.26 = (f32[1,1152]{1,0:T(1,128)S(1)}, f32[1,1152]{1,0:T(1,128)S(1)}, u32[]{:S(2)}, u32[]{:S(2)}) collective-permute-start(f32[1,1152]{1,0:T(1,128)S(1)} %copy-done.9), channel_id=1, source_target_pairs={{0,8},{1,9},{2,10},{3,11},{4,12},{5,13},{6,14},{7,15},{8,0},{9,1},... | collective-permute-start | bytes 13832 | tf_op jit(solution)/shard_map/ppermute | solution.py:422
  438.0 57.4 %collective-permute-start.15 = (bf16[4,2,2,288,240]{4,3,2,1,0:T(8,128)(2,1)}, bf16[4,2,2,288,240]{4,3,2,1,0:T(8,128)(2,1)S(1)}, u32[]{:S(2)}, u32[]{:S(2)}) collective-permute-start(bf16[4,2,2,288,240]{4,3,2,1,0:T(8,128)(2,1)} %get-tuple-element.122), channel_id=1, source_target_pairs={{0,8},{1,9},{2,10},{3,11},{4,12},{5,13},{6,14},{7,15},{8,0},{9,1},... | collective-permute-start | bytes 6635528 | tf_op jit(solution)/shard_map/ppermute | solution.py:422
  441.5 21.0 %collective-permute-start.32 = (bf16[4,288,384]{2,1,0:T(8,128)(2,1)S(1)}, bf16[4,288,384]{2,1,0:T(8,128)(2,1)S(1)}, u32[]{:S(2)}, u32[]{:S(2)}) collective-permute-start(bf16[4,288,384]{2,1,0:T(8,128)(2,1)S(1)} %fusion.8), channel_id=1, source_target_pairs={{0,1},{1,0},{2,3},{3,2},{4,5},{5,4},{6,7},{7,6},{8,9},{9,8},{10,11... | collective-permute-start | bytes 2654216 | tf_op jit(solution)/shard_map/ppermute | solution.py:422
  444.3 22.7 %collective-permute-start.37 = (bf16[4,288,384]{2,1,0:T(8,128)(2,1)S(1)}, bf16[4,288,384]{2,1,0:T(8,128)(2,1)S(1)}, u32[]{:S(2)}, u32[]{:S(2)}) collective-permute-start(bf16[4,288,384]{2,1,0:T(8,128)(2,1)S(1)} %fusion.10), channel_id=1, source_target_pairs={{0,16},{1,17},{2,18},{3,19},{4,20},{5,21},{6,22},{7,23},{8,24},{9,... | collective-permute-start | bytes 2654216 | tf_op jit(solution)/shard_map/ppermute | solution.py:422
  447.2 46.4 %collective-permute-start.22 = (bf16[4,144,1056]{2,1,0:T(8,128)(2,1)S(1)}, bf16[4,144,1056]{2,1,0:T(8,128)(2,1)S(1)}, u32[]{:S(2)}, u32[]{:S(2)}) collective-permute-start(bf16[4,144,1056]{2,1,0:T(8,128)(2,1)S(1)} %fusion.4), channel_id=1, source_target_pairs={{0,16},{1,17},{2,18},{3,19},{4,20},{5,21},{6,22},{7,23},{8,24},{9,... | collective-permute-start | bytes 3649544 | tf_op jit(solution)/shard_map/ppermute | solution.py:422
  464.1 8.4 %collective-permute-start.33 = (bf16[288,384]{1,0:T(8,128)(2,1)S(1)}, bf16[288,384]{1,0:T(8,128)(2,1)S(1)}, u32[]{:S(2)}, u32[]{:S(2)}) collective-permute-start(bf16[288,384]{1,0:T(8,128)(2,1)S(1)} %slice_bitcast_fusion.15), channel_id=1, source_target_pairs={{0,6},{1,7},{2,0},{3,1},{4,2},{5,3},{6,4},{7,5},{8,14},{9,15},{10,... | collective-permute-start | bytes 663560 | tf_op jit(solution)/shard_map/ppermute | solution.py:422
  468.5 8.7 %collective-permute-start.38 = (bf16[288,384]{1,0:T(8,128)(2,1)S(1)}, bf16[288,384]{1,0:T(8,128)(2,1)S(1)}, u32[]{:S(2)}, u32[]{:S(2)}) collective-permute-start(bf16[288,384]{1,0:T(8,128)(2,1)S(1)} %slice_bitcast_fusion.11), channel_id=1, source_target_pairs={{0,6},{1,7},{2,0},{3,1},{4,2},{5,3},{6,4},{7,5},{8,14},{9,15},{10,... | collective-permute-start | bytes 663560 | tf_op jit(solution)/shard_map/ppermute | solution.py:422
  472.5 9.4 %collective-permute-start.34 = (bf16[288,384]{1,0:T(8,128)(2,1)S(1)}, bf16[288,384]{1,0:T(8,128)(2,1)S(1)}, u32[]{:S(2)}, u32[]{:S(2)}) collective-permute-start(bf16[288,384]{1,0:T(8,128)(2,1)S(1)} %fusion.24), channel_id=1, source_target_pairs={{0,6},{1,7},{2,0},{3,1},{4,2},{5,3},{6,4},{7,5},{8,14},{9,15},{10,... | collective-permute-start | bytes 663560 | tf_op jit(solution)/shard_map/ppermute | solution.py:422
  477.2 20.8 %collective-permute-start.39 = (bf16[288,384]{1,0:T(8,128)(2,1)S(1)}, bf16[288,384]{1,0:T(8,128)(2,1)S(1)}, u32[]{:S(2)}, u32[]{:S(2)}) collective-permute-start(bf16[288,384]{1,0:T(8,128)(2,1)S(1)} %fusion.22), channel_id=1, source_target_pairs={{0,6},{1,7},{2,0},{3,1},{4,2},{5,3},{6,4},{7,5},{8,14},{9,15},{10,... | collective-permute-start | bytes 663560 | tf_op jit(solution)/shard_map/ppermute | solution.py:422
  482.0 17.2 %collective-permute-start.35 = (bf16[288,384]{1,0:T(8,128)(2,1)S(1)}, bf16[288,384]{1,0:T(8,128)(2,1)S(1)}, u32[]{:S(2)}, u32[]{:S(2)}) collective-permute-start(bf16[288,384]{1,0:T(8,128)(2,1)S(1)} %fusion.25), channel_id=1, source_target_pairs={{0,6},{1,7},{2,0},{3,1},{4,2},{5,3},{6,4},{7,5},{8,14},{9,15},{10,... | collective-permute-start | bytes 663560 | tf_op jit(solution)/shard_map/ppermute | solution.py:422
  496.3 26.3 %collective-permute-start.16 = (bf16[4,2,288,240]{3,2,1,0:T(8,128)(2,1)S(1)}, bf16[4,2,288,240]{3,2,1,0:T(8,128)(2,1)S(1)}, u32[]{:S(2)}, u32[]{:S(2)}) collective-permute-start(bf16[4,2,288,240]{3,2,1,0:T(8,128)(2,1)S(1)} %get-tuple-element.156), channel_id=1, source_target_pairs={{0,16},{1,17},{2,18},{3,19},{4,20},{5,21},{6,22},{7,23},{8,24},{9,... | collective-permute-start | bytes 3317768 | tf_op jit(solution)/shard_map/ppermute | solution.py:422
  496.8 10.8 %collective-permute-start.23 = (bf16[144,1056]{1,0:T(8,128)(2,1)S(1)}, bf16[144,1056]{1,0:T(8,128)(2,1)S(1)}, u32[]{:S(2)}, u32[]{:S(2)}) collective-permute-start(bf16[144,1056]{1,0:T(8,128)(2,1)S(1)} %slice_bitcast_fusion.7), channel_id=1, source_target_pairs={{0,6},{1,7},{2,0},{3,1},{4,2},{5,3},{6,4},{7,5},{8,14},{9,15},{10,... | collective-permute-start | bytes 912392 | tf_op jit(solution)/shard_map/ppermute | solution.py:422
  498.0 25.5 %collective-permute-start.40 = (bf16[288,384]{1,0:T(8,128)(2,1)S(1)}, bf16[288,384]{1,0:T(8,128)(2,1)S(1)}, u32[]{:S(2)}, u32[]{:S(2)}) collective-permute-start(bf16[288,384]{1,0:T(8,128)(2,1)S(1)} %fusion.23), channel_id=1, source_target_pairs={{0,6},{1,7},{2,0},{3,1},{4,2},{5,3},{6,4},{7,5},{8,14},{9,15},{10,... | collective-permute-start | bytes 663560 | tf_op jit(solution)/shard_map/ppermute | solution.py:422
  507.7 16.7 %collective-permute-start.24 = (bf16[144,1056]{1,0:T(8,128)(2,1)S(1)}, bf16[144,1056]{1,0:T(8,128)(2,1)S(1)}, u32[]{:S(2)}, u32[]{:S(2)}) collective-permute-start(bf16[144,1056]{1,0:T(8,128)(2,1)S(1)} %fusion.18), channel_id=1, source_target_pairs={{0,6},{1,7},{2,0},{3,1},{4,2},{5,3},{6,4},{7,5},{8,14},{9,15},{10,... | collective-permute-start | bytes 912392 | tf_op jit(solution)/shard_map/ppermute | solution.py:422
  522.8 12.7 %collective-permute-start.17 = (bf16[4,288,240]{2,1,0:T(8,128)(2,1)S(1)}, bf16[4,288,240]{2,1,0:T(8,128)(2,1)S(1)}, u32[]{:S(2)}, u32[]{:S(2)}) collective-permute-start(bf16[4,288,240]{2,1,0:T(8,128)(2,1)S(1)} %fusion.21), channel_id=1, source_target_pairs={{0,1},{1,0},{2,3},{3,2},{4,5},{5,4},{6,7},{7,6},{8,9},{9,8},{10,11... | collective-permute-start | bytes 1658888 | tf_op jit(solution)/shard_map/ppermute | solution.py:422
  524.5 11.3 %collective-permute-start.25 = (bf16[144,1056]{1,0:T(8,128)(2,1)S(1)}, bf16[144,1056]{1,0:T(8,128)(2,1)S(1)}, u32[]{:S(2)}, u32[]{:S(2)}) collective-permute-start(bf16[144,1056]{1,0:T(8,128)(2,1)S(1)} %fusion.19), channel_id=1, source_target_pairs={{0,6},{1,7},{2,0},{3,1},{4,2},{5,3},{6,4},{7,5},{8,14},{9,15},{10,... | collective-permute-start | bytes 912392 | tf_op jit(solution)/shard_map/ppermute | solution.py:422
  535.7 6.4 %collective-permute-start.18 = (bf16[288,240]{1,0:T(8,128)(2,1)S(1)}, bf16[288,240]{1,0:T(8,128)(2,1)S(1)}, u32[]{:S(2)}, u32[]{:S(2)}) collective-permute-start(bf16[288,240]{1,0:T(8,128)(2,1)S(1)} %slice_bitcast_fusion.20), channel_id=1, source_target_pairs={{0,6},{1,7},{2,0},{3,1},{4,2},{5,3},{6,4},{7,5},{8,14},{9,15},{10,... | collective-permute-start | bytes 414728 | tf_op jit(solution)/shard_map/ppermute | solution.py:422
  542.1 5.6 %collective-permute-start.19 = (bf16[288,240]{1,0:T(8,128)(2,1)S(1)}, bf16[288,240]{1,0:T(8,128)(2,1)S(1)}, u32[]{:S(2)}, u32[]{:S(2)}) collective-permute-start(bf16[288,240]{1,0:T(8,128)(2,1)S(1)} %fusion.26), channel_id=1, source_target_pairs={{0,6},{1,7},{2,0},{3,1},{4,2},{5,3},{6,4},{7,5},{8,14},{9,15},{10,... | collective-permute-start | bytes 414728 | tf_op jit(solution)/shard_map/ppermute | solution.py:422
  547.8 5.8 %collective-permute-start.20 = (bf16[288,240]{1,0:T(8,128)(2,1)S(1)}, bf16[288,240]{1,0:T(8,128)(2,1)S(1)}, u32[]{:S(2)}, u32[]{:S(2)}) collective-permute-start(bf16[288,240]{1,0:T(8,128)(2,1)S(1)} %fusion.27), channel_id=1, source_target_pairs={{0,6},{1,7},{2,0},{3,1},{4,2},{5,3},{6,4},{7,5},{8,14},{9,15},{10,... | collective-permute-start | bytes 414728 | tf_op jit(solution)/shard_map/ppermute | solution.py:422
  (19 other events, 298.9 us)
